TPU v7x, 128 devices: a whole 4x4x4 slice. The times are simulated.
128 devices in a mesh: major: 8 (over x_lo, y), minor: 16 (over z, x_hi, core).
Axes of the slice: x: 4 (x_hi: 2, x_lo: 2; x = x_hi * 2 + x_lo), y: 4, z: 4, core: 2. Of those that a mesh axis runs over, the one named last changes fastest.
Arguments:
- block_in: bfloat16 [16384, 1024], P(('major', 'minor')), may hold values from -24 to 24
- out_cot: bfloat16 [16384, 1024], P(('major', 'minor')), may hold values from -6 to 6
- w_in: bfloat16 [1024, 3072], replicated, may hold values from -0.1875 to 0.1875
- w_out: bfloat16 [1024, 1024], replicated, may hold values from -0.1875 to 0.1875
- conv_one: bfloat16 [16384, 1024], P(('major', 'minor')), may hold values from -6 to 6
- conv_two: bfloat16 [16384, 1024], P(('major', 'minor')), may hold values from -6 to 6
- filter_one: bfloat16 [16384, 1024], P(('major', 'minor')), may hold values from -6 to 6
- filter_two: bfloat16 [16384, 1024], P(('major', 'minor')), may hold values from -6 to 6
Outputs:
- in_grad: bfloat16 [16384, 1024], P(('major', 'minor'))
- w_in_grad: float32 [1024, 3072], P(('major', 'minor'))
- w_out_grad: float32 [1024, 1024], P(('major', 'minor'))
- filter_one_grad: bfloat16 [16384, 1024], P(('major', 'minor'))
- filter_two_grad: bfloat16 [16384, 1024], P(('major', 'minor'))
All inputs are finite; a program needn't handle non-finite values.
Results may differ from a plain program's by a relative error of at most 0.014.
Values may be sent and summed in bfloat16 or wider, within the bound.
A program may use at most 128 MiB of HBM per device.

v0:
```python
import math

import jax
import jax.numpy as jnp
from jax import lax
from jax.sharding import Mesh
from jax.sharding import PartitionSpec as P

MAJOR_MINOR = ("major_0", "major_1", "minor_0", "minor_1", "minor_2")


EXACT = lax.Precision.HIGHEST


def cut_along(shard, dim, size):
    lengths = shard.shape
    pieces = shard.reshape(*lengths[:dim], size, lengths[dim] // size, *lengths[dim + 1 :])
    return jnp.moveaxis(pieces, dim, 0)


def in_order(pieces, dim):
    pieces = jnp.moveaxis(pieces, 0, dim)
    lengths = pieces.shape
    return pieces.reshape(*lengths[:dim], lengths[dim] * lengths[dim + 1], *lengths[dim + 2 :])


def moved_by_axis(pieces, axes, sequence):
    inside = pieces.shape[1:]
    out = pieces.reshape(*(lax.axis_size(a) for a in axes), *inside)
    for k in sequence:
        out = lax.all_to_all(out, axes[k], k, k, tiled=True)
    return out.reshape(-1, *inside)


def two_step_exchange(shard, groups, sequence, split_dim, concat_dim):
    size = lax.axis_size(groups[0]) * lax.axis_size(groups[1])
    pieces = cut_along(shard, split_dim, size)
    return in_order(moved_by_axis(pieces, groups, sequence), concat_dim)


def sum_by_chip(shard, chips, core, dim):
    sizes = (lax.axis_size(chips), lax.axis_size(core))
    pieces = cut_along(shard, dim, sizes[0] * sizes[1])
    inside = pieces.shape[1:]
    pieces = pieces.reshape(*sizes, *inside).swapaxes(0, 1).reshape(-1, *inside)
    pieces = lax.psum_scatter(pieces, core, scatter_dimension=0, tiled=True)
    return lax.psum_scatter(pieces, chips, scatter_dimension=0, tiled=True)[0]


def apply_table(matrix, data, form):
    return jnp.einsum(form, matrix, data, precision=EXACT)


def product(left, right):
    return (left.astype(jnp.float32) * right.astype(jnp.float32)).astype(jnp.bfloat16)


def conj_times(left_re, left_im, right_re, right_im):
    return (left_re * right_re + left_im * right_im, left_re * right_im - left_im * right_re)


def spectral_move(moving):
    moved = lax.all_to_all(moving, MAJOR_MINOR, split_axis=2, concat_axis=2, tiled=True)
    return moved


def build_tables(rows_dev):
    devices = lax.axis_size(MAJOR_MINOR)
    index = lax.axis_index(MAJOR_MINOR)
    per_group = rows_dev // devices
    seq_len = rows_dev * devices
    grid = jnp.arange(devices, dtype=jnp.int32)
    line = jnp.arange(rows_dev, dtype=jnp.int32)
    local_pos = index * per_group + jnp.arange(per_group, dtype=jnp.int32)
    grid_angle = (
        -2.0 * math.pi * (grid[:, None] * grid[None, :] % devices).astype(jnp.float32) / devices
    )
    line_angle = (
        -2.0 * math.pi * (line[:, None] * line[None, :] % rows_dev).astype(jnp.float32) / rows_dev
    )
    steps_held = rows_dev * grid[:, None] + local_pos[None, :]
    seq_angle = -math.pi * steps_held.astype(jnp.float32) / seq_len
    turn_angle = (
        -2.0
        * math.pi
        * (grid[:, None] * local_pos[None, :] % seq_len).astype(jnp.float32)
        / seq_len
    )
    back_angle = 2.0 * math.pi * (line * index % seq_len).astype(jnp.float32) / seq_len
    return {
        "grid_cos": jnp.cos(grid_angle),
        "grid_sin": jnp.sin(grid_angle),
        "line_cos": jnp.cos(line_angle),
        "line_sin": jnp.sin(line_angle),
        "seq_cos": jnp.cos(seq_angle),
        "seq_sin": jnp.sin(seq_angle),
        "turn_cos": jnp.cos(turn_angle),
        "turn_sin": jnp.sin(turn_angle),
        "back_cos": jnp.cos(back_angle),
        "back_sin": jnp.sin(back_angle),
    }


def forward_spectrum(fields, tables):
    count, rows_dev, width = fields.shape
    devices = tables["grid_cos"].shape[0]
    per_group = rows_dev // devices
    pieces = fields.reshape(count, devices, per_group, width)
    landed = lax.all_to_all(pieces, MAJOR_MINOR, split_axis=1, concat_axis=1, tiled=True).astype(
        jnp.float32
    )
    twist_re = landed * tables["seq_cos"][None, :, :, None]
    twist_im = landed * tables["seq_sin"][None, :, :, None]
    form = "ka,fard->fkrd"
    grid_cos = tables["grid_cos"]
    grid_sin = tables["grid_sin"]
    even_re = apply_table(grid_cos, landed, form)
    even_im = apply_table(grid_sin, landed, form)
    odd_re = apply_table(grid_cos, twist_re, form) - apply_table(grid_sin, twist_im, form)
    odd_im = apply_table(grid_cos, twist_im, form) + apply_table(grid_sin, twist_re, form)
    part_re = jnp.stack([even_re, odd_re], axis=1)
    part_im = jnp.stack([even_im, odd_im], axis=1)
    turn_cos = tables["turn_cos"][None, None, :, :, None]
    turn_sin = tables["turn_sin"][None, None, :, :, None]
    moving = jnp.concatenate(
        [part_re * turn_cos - part_im * turn_sin, part_re * turn_sin + part_im * turn_cos], axis=1
    )
    arrived = spectral_move(moving).reshape(count, 4, rows_dev, width)
    line_re = arrived[:, :2]
    line_im = arrived[:, 2:]
    form_line = "kb,fcbd->fckd"
    line_cos = tables["line_cos"]
    line_sin = tables["line_sin"]
    out_re = apply_table(line_cos, line_re, form_line) - apply_table(line_sin, line_im, form_line)
    out_im = apply_table(line_cos, line_im, form_line) + apply_table(line_sin, line_re, form_line)
    return (out_re, out_im)


def inverse_field(spec_re, spec_im, factor, tables):
    count, _, rows_dev, width = spec_re.shape
    devices = tables["grid_cos"].shape[0]
    per_group = rows_dev // devices
    form_line = "bk,fckd->fcbd"
    line_cos = tables["line_cos"]
    line_sin = tables["line_sin"]
    back_re = apply_table(line_cos, spec_re, form_line) + apply_table(line_sin, spec_im, form_line)
    back_im = apply_table(line_cos, spec_im, form_line) - apply_table(line_sin, spec_re, form_line)
    turn_cos = tables["back_cos"][None, None, :, None]
    turn_sin = tables["back_sin"][None, None, :, None]
    moving = jnp.concatenate(
        [back_re * turn_cos - back_im * turn_sin, back_re * turn_sin + back_im * turn_cos], axis=1
    )
    moving = moving.reshape(count, 4, devices, per_group, width)
    moved = spectral_move(moving)
    head_re = moved[:, :2]
    head_im = moved[:, 2:]
    grid_cos = tables["grid_cos"]
    grid_sin = tables["grid_sin"]
    form_grid = "ak,fckrd->fcard"
    grid_re = apply_table(grid_cos, head_re, form_grid) + apply_table(grid_sin, head_im, form_grid)
    form_odd = "ak,fkrd->fard"
    odd_im = apply_table(grid_cos, head_im[:, 1], form_odd) - apply_table(
        grid_sin, head_re[:, 1], form_odd
    )
    seq_cos = tables["seq_cos"][None, :, :, None]
    seq_sin = tables["seq_sin"][None, :, :, None]
    total = ((grid_re[:, 0] + grid_re[:, 1] * seq_cos + odd_im * seq_sin) * factor).astype(
        jnp.bfloat16
    )
    returned = two_step_exchange(
        total, (("major_0", "major_1", "minor_0", "minor_1"), "minor_2"), (1, 0), 1, 2
    )
    return returned.reshape(count, rows_dev, width)


def shards(block_in, out_cot, w_in, w_out, conv_one, conv_two, filter_one, filter_two):
    rows_dev, width = block_in.shape
    devices = lax.axis_size(MAJOR_MINOR)
    seq_len = rows_dev * devices
    scale = seq_len ** (-0.5)
    factor = scale / (2.0 * seq_len)
    tables = build_tables(rows_dev)
    contract_last = (((1,), (1,)), ((), ()))
    contract_first = (((0,), (0,)), ((), ()))
    proj = jnp.dot(block_in, w_in, preferred_element_type=jnp.float32).astype(jnp.bfloat16)
    value = proj[:, :width]
    gate_one = proj[:, width : 2 * width]
    gate_two = proj[:, 2 * width :]
    first_out = product(gate_one, conv_one)
    second_out = product(gate_two, conv_two)
    grad_second = lax.dot_general(
        out_cot, w_out, contract_last, preferred_element_type=jnp.float32
    ).astype(jnp.bfloat16)
    grad_conv_two = product(grad_second, gate_two)
    grad_gate_two = product(grad_second, conv_two)
    spec_re, spec_im = forward_spectrum(
        jnp.stack([value, first_out, filter_one, filter_two, grad_conv_two]), tables
    )
    pair_re, pair_im = conj_times(
        jnp.stack([spec_re[3], spec_re[1]]),
        jnp.stack([spec_im[3], spec_im[1]]),
        spec_re[4][None],
        spec_im[4][None],
    )
    first_back = inverse_field(pair_re, pair_im, factor, tables)
    grad_first = first_back[0]
    filter_two_grad = first_back[1]
    grad_conv_one = product(grad_first, gate_one)
    grad_gate_one = product(grad_first, conv_one)
    single_re, single_im = forward_spectrum(grad_conv_one[None], tables)
    pair_re, pair_im = conj_times(
        jnp.stack([spec_re[2], spec_re[0]]),
        jnp.stack([spec_im[2], spec_im[0]]),
        single_re,
        single_im,
    )
    second_back = inverse_field(pair_re, pair_im, factor, tables)
    grad_value = second_back[0]
    filter_one_grad = second_back[1]
    grad_proj = jnp.concatenate([grad_value, grad_gate_one, grad_gate_two], axis=1)
    in_grad = lax.dot_general(
        grad_proj, w_in, contract_last, preferred_element_type=jnp.float32
    ).astype(jnp.bfloat16)
    in_part = lax.dot_general(
        block_in, grad_proj, contract_first, preferred_element_type=jnp.float32
    )
    out_part = lax.dot_general(
        second_out, out_cot, contract_first, preferred_element_type=jnp.float32
    )
    summed = (
        sum_by_chip(
            jnp.concatenate([in_part, out_part], axis=1),
            ("major_0", "major_1", "minor_0", "minor_1"),
            "minor_2",
            0,
        )
        * scale
    )
    return (
        in_grad,
        summed[:, : 3 * width],
        summed[:, 3 * width :],
        filter_one_grad,
        filter_two_grad,
    )


def solution(mesh):
    finer = Mesh(
        mesh.devices.reshape(2, 4, 4, 2, 2), ("major_0", "major_1", "minor_0", "minor_1", "minor_2")
    )
    placed = (
        P(MAJOR_MINOR, None),
        P(MAJOR_MINOR, None),
        P(),
        P(),
        P(MAJOR_MINOR, None),
        P(MAJOR_MINOR, None),
        P(MAJOR_MINOR, None),
        P(MAJOR_MINOR, None),
    )
    return jax.shard_map(
        shards,
        mesh=finer,
        in_specs=placed,
        out_specs=(
            P(MAJOR_MINOR, None),
            P(MAJOR_MINOR, None),
            P(MAJOR_MINOR, None),
            P(MAJOR_MINOR, None),
            P(MAJOR_MINOR, None),
        ),
        check_vma=False,
    )
```

profile of v0, /device:TPU:0, one launch (start us, length us, event | category | flops | bytes accessed | tf_op | source)
XLA Modules:
  0.0 1064.6 jit_solution(15636371205260168056)
XLA Ops:
  16.2 11.2 %all-to-all-start = ((bf16[5,128,1,1024]{3,0,2,1:T(8,128)(2,1)}), bf16[5,128,1,1024]{3,0,2,1:T(8,128)(2,1)S(1)}, u32[]{:S(2)}, u32[]{:S(2)}) async-start(bf16[5,128,1,1024]{3,0,2,1:T(8,128)(2,1)} %copy.144), calls=%async_computation | async-start | bytes 4194304 | tf_op jit(solution)/shard_map/all_to_all | solution.py:109
  27.5 29.4 %all-to-all-done = bf16[5,128,1,1024]{3,0,2,1:T(8,128)(2,1)S(1)} async-done(((bf16[5,128,1,1024]{3,0,2,1:T(8,128)(2,1)}), bf16[5,128,1,1024]{3,0,2,1:T(8,128)(2,1)S(1)}, u32[]{:S(2)}, u32[]{:S(2)}) %all-to-all-start) | async-done | bytes 1310752 | tf_op jit(solution)/shard_map/all_to_all | solution.py:109
  73.5 5.3 copy.147
  95.9 9.1 pad_maximum_fusion.1
  105.0 12.8 %copy.150 = f32[5,4,128,1,1024]{4,1,3,0,2:T(4,128)} copy(f32[5,4,128,1,1024]{2,4,0,3,1:T(8,128)} %pad_maximum_fusion.1) | data formatting | bytes 20971520 | tf_op jit(solution)/shard_map/concatenate | solution.py:125
  117.8 5.9 all-to-all-start.1
  123.7 128.3 %all-to-all-done.1 = f32[5,4,128,1,1024]{4,1,3,0,2:T(4,128)} async-done(((f32[5,4,128,1,1024]{4,1,3,0,2:T(4,128)}), f32[5,4,128,1,1024]{4,1,3,0,2:T(4,128)}, u32[]{:S(2)}, u32[]{:S(2)}) %all-to-all-start.1) | async-done | bytes 10485792 | tf_op jit(solution)/shard_map/all_to_all | solution.py:63
  252.0 12.4 %copy.151 = f32[5,4,128,1,1024]{2,4,1,0,3:T(8,128)} copy(f32[5,4,128,1,1024]{4,1,3,0,2:T(4,128)} %all-to-all-done.1) | data formatting | bytes 20971520 | tf_op jit(solution)/shard_map/all_to_all | solution.py:63
  264.4 7.1 fusion.4
  301.0 5.5 copy.152
  306.6 69.0 %all_to_all.50 = f32[2,4,128,1,1024]{4,1,0,3,2:T(4,128)S(1)} all-to-all(f32[2,4,128,1,1024]{4,1,0,3,2:T(4,128)} %copy.152), channel_id=1, replica_groups=mesh['major_0'=2,'major_1'=4,'minor_0'=4,'minor_1'=2,'minor_2'=2] {'majo..., dimensions={2} | all-to-all | bytes 8388608 | tf_op jit(solution)/shard_map/all_to_all | solution.py:63
  395.4 19.2 %all_to_all.52 = bf16[64,2,2,1,1,1024]{5,1,2,4,3,0:T(2,128)(2,1)S(1)} all-to-all(bf16[64,2,2,1,1,1024]{5,1,2,4,3,0:T(2,128)(2,1)S(1)} %copy.159), channel_id=1, replica_groups=mesh['major_0'=2,'major_1'=4,'minor_0'=4,'minor_1'=2,'minor_2'=2] {'majo..., dimensions={0} | all-to-all | bytes 1048576 | tf_op jit(solution)/shard_map/all_to_all | solution.py:31
  419.8 15.1 %all_to_all.53 = bf16[128,2,512]{2,1,0:T(2,128)(2,1)S(1)} all-to-all(bf16[128,2,512]{2,1,0:T(2,128)(2,1)S(1)} %reshape.619), channel_id=1, replica_groups=mesh['major_0'=2,'major_1'=4,'minor_0'=4,'minor_1'=2,'minor_2'=2] {'majo..., dimensions={0} | all-to-all | bytes 524288 | tf_op jit(solution)/shard_map/all_to_all | solution.py:109
  446.3 35.1 %all_to_all.54 = f32[1,4,128,1,1024]{4,3,1,0,2:T(1,128)} all-to-all(f32[1,4,128,1,1024]{4,3,1,0,2:T(1,128)} %copy.162), channel_id=1, replica_groups=mesh['major_0'=2,'major_1'=4,'minor_0'=4,'minor_1'=2,'minor_2'=2] {'majo..., dimensions={2} | all-to-all | bytes 4194304 | tf_op jit(solution)/shard_map/all_to_all | solution.py:63
  504.7 5.5 copy.164
  510.3 58.2 %all_to_all.55 = f32[2,4,128,1,1024]{4,1,0,3,2:T(4,128)S(1)} all-to-all(f32[2,4,128,1,1024]{4,1,0,3,2:T(4,128)} %copy.164), channel_id=1, replica_groups=mesh['major_0'=2,'major_1'=4,'minor_0'=4,'minor_1'=2,'minor_2'=2] {'majo..., dimensions={2} | all-to-all | bytes 8388608 | tf_op jit(solution)/shard_map/all_to_all | solution.py:63
  589.3 5.9 all-to-all-start.9
  598.9 9.8 all-to-all-done.9
  612.2 7.2 pad_maximum_fusion
  619.4 17.5 %copy.174 = f32[1024,4096]{1,0:T(8,128)} copy(f32[1024,4096]{0,1:T(8,128)} %pad_maximum_fusion) | data formatting | bytes 33554432 | tf_op jit(solution)/shard_map/concatenate | solution.py:232
  636.9 11.6 %copy.175 = f32[2,64,8,4096]{3,2,1,0:T(8,128)} copy(f32[2,64,8,4096]{3,2,0,1:T(8,128)} %bitcast.389) | data formatting | bytes 33554432 | tf_op jit(solution)/shard_map/transpose | solution.py:45
  648.5 23.6 %reduce-scatter.3.cloned.1.call-done = f32[64,8,4096]{2,1,0:T(8,128)} async-done(((f32[128,8,4096]{2,1,0:T(8,128)}), f32[64,8,4096]{2,1,0:T(8,128)}) %reduce-scatter.3.cloned.1.call-update) | async-done | bytes 8388624 | tf_op jit(solution)/shard_map/reduce_scatter | solution.py:46
  673.9 5.8 convolution_convert_fusion.1
  679.7 375.7 %reduce-scatter.5.cloned.1.call-done = f32[1,8,4096]{2,1,0:T(8,128)} async-done(((f32[64,8,4096]{2,1,0:T(8,128)}), f32[1,8,4096]{2,1,0:T(8,128)}) %reduce-scatter.5.cloned.1.call-update) | async-done | bytes 131088 | tf_op jit(solution)/shard_map/reduce_scatter | solution.py:47
  (144 shorter events, 163.3 us)
Async XLA Ops:
  7.2 4.3 copy-start
  7.2 4.1 copy-start.18
  7.2 4.2 copy-start.24
  7.2 4.2 copy-start.25
  11.2 2.9 copy-start.13
  16.2 40.7 %all-to-all-start = ((bf16[5,128,1,1024]{3,0,2,1:T(8,128)(2,1)}), bf16[5,128,1,1024]{3,0,2,1:T(8,128)(2,1)S(1)}, u32[]{:S(2)}, u32[]{:S(2)}) async-start(bf16[5,128,1,1024]{3,0,2,1:T(8,128)(2,1)} %copy.144), calls=%async_computation | async-start | bytes 4194304 | tf_op jit(solution)/shard_map/all_to_all | solution.py:109
  78.9 4.5 copy-start.6
  85.9 2.6 copy-start.7
  88.5 2.6 copy-start.11
  88.5 2.6 copy-start.12
  117.8 134.3 %all-to-all-start.1 = ((f32[5,4,128,1,1024]{4,1,3,0,2:T(4,128)}), f32[5,4,128,1,1024]{4,1,3,0,2:T(4,128)}, u32[]{:S(2)}, u32[]{:S(2)}) async-start(f32[5,4,128,1,1024]{4,1,3,0,2:T(4,128)} %copy.150), calls=%async_computation.1 | async-start | bytes 20971520 | tf_op jit(solution)/shard_map/all_to_all | solution.py:63
  264.4 7.2 copy-start.2
  394.9 20.3 %copy-start.19 = (bf16[128,1024]{1,0:T(8,128)(2,1)S(1)}, bf16[128,1024]{1,0:T(8,128)(2,1)}, u32[]{:S(2)}) copy-start(bf16[128,1024]{1,0:T(8,128)(2,1)} %param.12) | copy-start | bytes 786436
  415.2 19.9 %copy-start.14 = (bf16[128,2,1,1,1024]{4,0,3,2,1:T(8,128)(2,1)}, bf16[128,2,1,1,1024]{4,0,3,2,1:T(8,128)(2,1)S(1)}, u32[]{:S(2)}) copy-start(bf16[128,2,1,1,1024]{4,0,3,2,1:T(8,128)(2,1)S(1)} %reshape.598) | copy-start | bytes 1572868
  488.8 2.6 copy-start.9
  583.5 11.7 %copy-start.21 = (bf16[128,1024]{1,0:T(8,128)(2,1)S(1)}, bf16[128,1024]{1,0:T(8,128)(2,1)}, u32[]{:S(2)}) copy-start(bf16[128,1024]{1,0:T(8,128)(2,1)} %param.13) | copy-start | bytes 786436
  583.5 11.7 %copy-start.23 = (bf16[128,1024]{1,0:T(8,128)(2,1)S(1)}, bf16[128,1024]{1,0:T(8,128)(2,1)}, u32[]{:S(2)}) copy-start(bf16[128,1024]{1,0:T(8,128)(2,1)} %param.9) | copy-start | bytes 786436
  589.3 19.4 %all-to-all-start.9 = ((bf16[64,2,2,1,1,1024]{5,1,2,4,3,0:T(2,128)(2,1)}), bf16[64,2,2,1,1,1024]{5,1,2,4,3,0:T(2,128)(2,1)S(1)}, u32[]{:S(2)}, u32[]{:S(2)}) async-start(bf16[64,2,2,1,1,1024]{5,1,2,4,3,0:T(2,128)(2,1)} %copy.172), calls=%async_computation.9 | async-start | bytes 1048576 | tf_op jit(solution)/shard_map/all_to_all | solution.py:31
  595.1 77.0 %reduce-scatter.3.cloned.1.call-start = ((), (), s32[]{:S(2)}) async-start(), calls=%async_computation.12 | async-start | bytes 25165824 | tf_op jit(solution)/shard_map/reduce_scatter | solution.py:46
  598.9 11.1 %copy-start.16 = (bf16[128,1024]{1,0:T(8,128)(2,1)S(1)}, bf16[128,1024]{1,0:T(8,128)(2,1)}, u32[]{:S(2)}) copy-start(bf16[128,1024]{1,0:T(8,128)(2,1)} %param.8) | copy-start | bytes 786436
  598.9 11.1 %copy-start.17 = (bf16[128,1024]{1,0:T(8,128)(2,1)S(1)}, bf16[128,1024]{1,0:T(8,128)(2,1)}, u32[]{:S(2)}) copy-start(bf16[128,1024]{1,0:T(8,128)(2,1)} %get-tuple-element.39) | copy-start | bytes 786436
  610.0 2.2 copy-start.10
  648.5 407.0 %reduce-scatter.5.cloned.1.call-start = ((), (), s32[]{:S(2)}) async-start(), calls=%async_computation.13 | async-start | bytes 8519680 | tf_op jit(solution)/shard_map/reduce_scatter | solution.py:47
  673.9 383.7 %copy-start.1 = (bf16[1024,1024]{1,0:T(8,128)(2,1)S(1)}, bf16[1024,1024]{1,0:T(8,128)(2,1)}, u32[]{:S(2)}) copy-start(bf16[1024,1024]{1,0:T(8,128)(2,1)} %param.11) | copy-start | bytes 6291460
  (7 other events, 9.5 us)
Sparse Core Ops, SparseCore 0:
  648.6 23.4 reduce-scatter.2
  674.5 380.8 reduce-scatter.4
where the time goes:
time: 1070 us; the launch traced here: 1060 us
  waiting for transfers between devices  567 us (53%)
  blocking collectives  205 us (19%)
  local copies, waits for them, and re-layouts  110 us (10%)
  matrix products  109 us (10%)
  other arithmetic  35.4 us (3%)
  starting transfers between devices  23 us (2%)
  between operations  15 us (1%)
    reduce_scatter x1, waiting for transfers between devices, sum_by_chip(): return lax.psum_scatter(pieces, chips, scatter_dimension=0, tiled=True)[0]  376 us
    all_to_all x3, blocking collectives, spectral_move(): lax.all_to_all(moving, MAJOR_MINOR, split_axis=2, concat_axis=2, tiled=True)  162 us
    all_to_all x1, waiting for transfers between devices, spectral_move(): lax.all_to_all(moving, MAJOR_MINOR, split_axis=2, concat_axis=2, tiled=True)  128 us
    dot_general x36, matrix products, apply_table(): return jnp.einsum(form, matrix, data, precision=EXACT)  92 us
    all_to_all x1, waiting for transfers between devices, forward_spectrum(): lax.all_to_all(pieces, MAJOR_MINOR, split_axis=1, concat_axis=1, tiled=True)  29.4 us
    all_to_all x3, blocking collectives, moved_by_axis(): out = lax.all_to_all(out, axes[k], k, k, tiled=True)  27.6 us
    reduce_scatter x1, waiting for transfers between devices, sum_by_chip(): pieces = lax.psum_scatter(pieces, core, scatter_dimension=0, tiled=True)  23.6 us
  transfers between devices with their start and end apart: 5, of which 5 were waited for; matrix products, arithmetic and copies ran while one was open for 1% of the time, Pallas kernels for 0%

commit v1 on v0

v1 whole, which is shorter than its diff:
```python
import functools

import jax
import jax.numpy as jnp
import numpy as np
from jax import lax
from jax.experimental import pallas as pl
from jax.experimental.pallas import tpu as pltpu
from jax.sharding import PartitionSpec as P

AXES = ("major", "minor")
DEV = 128
CH = 8
LANES = 128
BF = jnp.bfloat16
F32 = jnp.float32
VALUE, GATE_ONE, CONV_ONE, FILTER_ONE, FILTER_TWO, GRAD_CONV_TWO = range(6)
FIELDS_IN = 6
FIELDS_OUT = 4


def dft_tables():
    k1 = np.arange(256)[:, None]
    n1 = np.arange(128)[None, :]
    a = 2.0 * np.pi * ((k1 * n1) % 256) / 256
    c, s = np.cos(a), np.sin(a)
    n2 = np.arange(128)
    b = 2.0 * np.pi * ((n2[:, None] * n2[None, :]) % 128) / 128
    cb, sb = np.cos(b), np.sin(b)
    t = 2.0 * np.pi * (k1 * n2[None, :]) / 32768
    return (
        np.block([[c, -s], [-s, -c]]).astype(BF),
        np.block([[c.T, -s.T], [s.T, c.T]]).astype(BF),
        np.block([[cb, -sb], [sb, cb]]).astype(BF),
        np.block([[cb, sb], [-sb, cb]]).astype(BF),
        np.stack([np.cos(t), np.sin(t)]).astype(np.float32),
    )


def round_mul(a, b):
    return (a * b).astype(BF).astype(F32)


def spectrum_of(data, table, line, tw_re, tw_im):
    grid = jnp.dot(table, data, preferred_element_type=F32)
    out = []
    for h in range(2):
        re = grid[:256, h * 128 : h * 128 + 128]
        im = grid[256:, h * 128 : h * 128 + 128]
        turned = jnp.concatenate([re * tw_re + im * tw_im, im * tw_re - re * tw_im], axis=1)
        out.append(jnp.dot(turned.astype(BF), line, preferred_element_type=F32))
    return out


def correlations(left, pair, refs, factor):
    fwd, inv, line, line_back, turn = refs
    tw_re, tw_im = turn[0], turn[1]
    specs = spectrum_of(left.astype(BF), fwd[:, :128], line[...], tw_re, tw_im)
    packs = spectrum_of(pair.astype(BF), fwd[...], line[...], tw_re, tw_im)
    backs_re, backs_im = [], []
    for spec, pack in zip(specs, packs):
        l_re, l_im = spec[:, :128], spec[:, 128:]
        p_re, p_im = pack[:, :128], pack[:, 128:]
        both = jnp.concatenate([l_re * p_re + l_im * p_im, l_im * p_re - l_re * p_im], axis=1)
        back = jnp.dot(both.astype(BF), line_back[...], preferred_element_type=F32)
        b_re, b_im = back[:, :128], back[:, 128:]
        backs_re.append(b_re * tw_re - b_im * tw_im)
        backs_im.append(b_re * tw_im + b_im * tw_re)
    stacked = jnp.concatenate(
        [jnp.concatenate(backs_re, axis=1), jnp.concatenate(backs_im, axis=1)], axis=0
    ).astype(BF)
    out = jnp.dot(inv[...], stacked, preferred_element_type=F32) * factor
    return out[:128].astype(BF).astype(F32), out[128:].astype(BF).astype(F32)


def local_kernel(factor, x_ref, fwd, inv, line, line_back, turn, o_ref, wide, narrow):
    wide[...] = x_ref[...].astype(F32)
    refs = (fwd, inv, line, line_back, turn)

    def pull(field, c):
        return jnp.concatenate(
            [wide[pl.ds(field * CH + c + h, DEV, FIELDS_IN * CH), :] for h in range(2)], axis=1
        )

    def push(field, c, data):
        for h in range(2):
            narrow[pl.ds(field * CH + c + h, DEV, FIELDS_OUT * CH), :] = data[
                :, h * 128 : h * 128 + 128
            ]

    def step(i, carry):
        c = 2 * i
        gate, conv = pull(GATE_ONE, c), pull(CONV_ONE, c)
        first_out = round_mul(gate, conv)
        grad_first, filter_two_grad = correlations(
            pull(GRAD_CONV_TWO, c),
            jnp.concatenate([pull(FILTER_TWO, c), first_out], axis=0),
            refs,
            factor,
        )
        push(1, c, round_mul(grad_first, conv))
        push(3, c, filter_two_grad)
        grad_value, filter_one_grad = correlations(
            round_mul(grad_first, gate),
            jnp.concatenate([pull(FILTER_ONE, c), pull(VALUE, c)], axis=0),
            refs,
            factor,
        )
        push(0, c, grad_value)
        push(2, c, filter_one_grad)
        return carry

    lax.fori_loop(0, CH // 2, step, 0)
    o_ref[...] = narrow[...].astype(BF)


def local_part(arrived, factor):
    tables = [jnp.asarray(t) for t in dft_tables()]
    flat = arrived.reshape(DEV * FIELDS_IN * CH, LANES)
    vmem = pl.BlockSpec(memory_space=pltpu.VMEM)
    out = pl.pallas_call(
        functools.partial(local_kernel, factor),
        out_shape=jax.ShapeDtypeStruct((DEV * FIELDS_OUT * CH, LANES), BF),
        in_specs=[vmem] * 6,
        out_specs=vmem,
        scratch_shapes=[
            pltpu.VMEM((DEV * FIELDS_IN * CH, LANES), F32),
            pltpu.VMEM((DEV * FIELDS_OUT * CH, LANES), F32),
        ],
        compiler_params=pltpu.CompilerParams(vmem_limit_bytes=56 << 20),
        name="local_part",
    )(flat, *tables)
    return out.reshape(DEV, FIELDS_OUT * CH, LANES)


def product(left, right):
    return (left.astype(F32) * right.astype(F32)).astype(BF)


def exchange(pieces):
    return lax.all_to_all(pieces, AXES, split_axis=0, concat_axis=0, tiled=True)


def shards(block_in, out_cot, w_in, w_out, conv_one, conv_two, filter_one, filter_two):
    rows, width = block_in.shape
    seq_len = rows * DEV
    scale = seq_len ** (-0.5)
    factor = scale / (2.0 * seq_len)
    contract_last = (((1,), (1,)), ((), ()))
    contract_first = (((0,), (0,)), ((), ()))
    proj = jnp.dot(block_in, w_in, preferred_element_type=F32).astype(BF)
    value, gate_one, gate_two = (proj[:, i * width : (i + 1) * width] for i in range(3))
    second_out = product(gate_two, conv_two)
    grad_second = lax.dot_general(
        out_cot, w_out, contract_last, preferred_element_type=F32
    ).astype(BF)
    grad_conv_two = product(grad_second, gate_two)
    grad_gate_two = product(grad_second, conv_two)
    fields = jnp.stack([value, gate_one, conv_one, filter_one, filter_two, grad_conv_two])
    fields = fields.reshape(FIELDS_IN, rows, DEV, CH).transpose(2, 0, 3, 1)
    arrived = exchange(fields.reshape(DEV, FIELDS_IN * CH, rows))
    back = exchange(local_part(arrived, factor)).reshape(DEV, FIELDS_OUT, CH, rows)
    back = back.transpose(1, 3, 0, 2).reshape(FIELDS_OUT, rows, width)
    grad_value, grad_gate_one, filter_one_grad, filter_two_grad = back
    grad_proj = jnp.concatenate([grad_value, grad_gate_one, grad_gate_two], axis=1)
    in_grad = lax.dot_general(
        grad_proj, w_in, contract_last, preferred_element_type=F32
    ).astype(BF)
    in_part = lax.dot_general(block_in, grad_proj, contract_first, preferred_element_type=F32)
    out_part = lax.dot_general(second_out, out_cot, contract_first, preferred_element_type=F32)
    parts = jnp.concatenate([in_part, out_part], axis=1).astype(BF)
    parts = exchange(parts.reshape(DEV, width // DEV, 4 * width))
    summed = jnp.sum(parts.astype(F32), axis=0) * scale
    return (
        in_grad,
        summed[:, : 3 * width],
        summed[:, 3 * width :],
        filter_one_grad,
        filter_two_grad,
    )


def solution(mesh):
    rows = P(AXES, None)
    return jax.shard_map(
        shards,
        mesh=mesh,
        in_specs=(rows, rows, P(), P(), rows, rows, rows, rows),
        out_specs=(rows,) * 5,
        check_vma=False,
    )
```

time: 1070 us -> 226 us (0.21)
  the two profiles are of different devices: /device:TPU:0 before, /device:TPU:1 now
where the time goes in v1:
time: 226 us; the launch traced here: 224 us
  waiting for transfers between devices  113 us (50%)
  blocking collectives  36.1 us (16%)
  local copies, waits for them, and re-layouts  20.8 us (9%)
  matrix products  18.7 us (8%)
  Pallas kernels  12.6 us (6%)
  other arithmetic  12.1 us (5%)
  starting transfers between devices  10.2 us (5%)
    all_to_all x2, waiting for transfers between devices, exchange(): return lax.all_to_all(pieces, AXES, split_axis=0, concat_axis=0, tiled=True)  113 us
    all_to_all x1, blocking collectives, exchange(): return lax.all_to_all(pieces, AXES, split_axis=0, concat_axis=0, tiled=True)  36.1 us
    pallas_call x1, Pallas kernels, local_part(): pl.pallas_call(functools.partial(local_kernel, factor), out_shape=jax.Sha...  12.6 us
    all_to_all x2, starting transfers between devices, exchange(): return lax.all_to_all(pieces, AXES, split_axis=0, concat_axis=0, tiled=True)  10.2 us
    unnamed x28, local copies, waits for them, and re-layouts  9.66 us
    concatenate x1, other arithmetic, shards(): parts = jnp.concatenate([in_part, out_part], axis=1).astype(BF)  7.56 us
    dot_general x1, matrix products, shards(): lax.dot_general(grad_proj, w_in, contract_last, preferred_element_type=F32)  5.68 us
    reduce_sum x1, other arithmetic, shards(): summed = jnp.sum(parts.astype(F32), axis=0) * scale  4.56 us
  transfers between devices with their start and end apart: 2, of which 2 were waited for; matrix products, arithmetic and copies ran while one was open for 5% of the time, Pallas kernels for 0%

profile of v1, /device:TPU:1, one launch (start us, length us, event | category | flops | bytes accessed | tf_op | source)
XLA Modules:
  0.0 223.8 jit_solution(425853382561507198)
XLA Ops:
  0.7 1.9 copy.32
  2.6 1.8 copy.33
  4.4 1.1 copy.34
  5.5 3.8 %convolution_convert_fusion = bf16[128,3072]{1,0:T(8,128)(2,1)S(1)} fusion(bf16[128,1024]{1,0:T(8,128)(2,1)S(1)} %copy-done.1, bf16[1024,3072]{1,0:T(8,128)(2,1)} %param.15), kind=kOutput, calls=%fused_computation.3 | convolution fusion | flops 805699584 | bytes 7340032 | tf_op jit(solution)/shard_map/dot_general | solution.py:151
  10.2 1.6 fusion.1
  11.9 1.8 copy.35
  13.7 1.8 copy.31
  15.5 1.8 copy.30
  17.3 1.0 bitcast_dynamic-update-slice_fusion.5
  18.3 1.0 bitcast_dynamic-update-slice_fusion.4
  19.3 1.0 bitcast_dynamic-update-slice_fusion.3
  20.7 36.1 %all_to_all.15 = bf16[128,48,128]{2,1,0:T(8,128)(2,1)} all-to-all(bf16[128,48,128]{2,1,0:T(8,128)(2,1)S(1)} %copy_bitcast_fusion), channel_id=1, replica_groups=mesh['major'=8,'minor'=16] {'major','minor'}, dimensions={0} | all-to-all | bytes 3145728 | tf_op jit(solution)/shard_map/all_to_all | solution.py:141
  56.8 12.6 %local_part.1 = bf16[4096,128]{1,0:T(8,128)(2,1)} custom-call(bf16[6144,128]{1,0:T(8,128)(2,1)} %bitcast.43, bf16[512,256]{1,0:T(8,128)(2,1)} %constant.14.clone.fwd, bf16[256,512]{1,0:T(8,128)(2,1)} %constant.15.clone.inv, bf16[256,256]{1,0:T(8,128)(2,1)} %constant.16.clone.line, bf16[256,256]{1,0:T(8,128)(2,1)} %constant.17.clone.line_back, ...), custom_call_target="tpu_custom_call" | custom-call | tf_op jit(solution)/shard_map/local_part/pallas_call | solution.py:121
  69.4 5.0 %all-to-all-start.1 = ((bf16[128,32,128]{2,1,0:T(8,128)(2,1)}), bf16[128,32,128]{2,1,0:T(8,128)(2,1)}, u32[]{:S(2)}, u32[]{:S(2)}) async-start(bf16[128,32,128]{2,1,0:T(8,128)(2,1)} %bitcast.44), calls=%async_computation.1 | async-start | bytes 2097152 | tf_op jit(solution)/shard_map/all_to_all | solution.py:141
  74.4 3.0 %convert_bitcast_fusion.1 = bf16[128,8,1024]{2,1,0:T(8,128)(2,1)} fusion(bf16[128,1024]{1,0:T(8,128)(2,1)} %param.14, bf16[128,1024]{1,0:T(8,128)(2,1)S(1)} %copy-done.7, bf16[128,3072]{1,0:T(8,128)(2,1)S(1)} %convolution_convert_fusion), kind=kOutput, calls=%fused_computation.4 | convolution fusion | flops 270008320 | bytes 2883584 | tf_op jit(solution)/shard_map/dot_general | solution.py:170
  77.4 15.9 %all-to-all-done.1 = bf16[128,32,128]{2,1,0:T(8,128)(2,1)} async-done(((bf16[128,32,128]{2,1,0:T(8,128)(2,1)}), bf16[128,32,128]{2,1,0:T(8,128)(2,1)}, u32[]{:S(2)}, u32[]{:S(2)}) %all-to-all-start.1) | async-done | bytes 1048608 | tf_op jit(solution)/shard_map/all_to_all | solution.py:141
  93.3 2.1 slice_bitcast_fusion
  95.6 1.1 copy.37
  96.7 4.5 %convert_bitcast_fusion = bf16[128,8,3072]{2,1,0:T(8,128)(2,1)} fusion(bf16[128,1024]{1,0:T(8,128)(2,1)S(1)} %copy-done.1, bf16[128,1024]{1,0:T(8,128)(2,1)S(1)} %copy-done.4, bf16[128,1024]{1,0:T(8,128)(2,1)S(1)} %copy.38, bf16[128,1024]{1,0:T(8,128)(2,1)S(1)} %copy.37), kind=kOutput, calls=%fused_computation.2 | convolution fusion | flops 810811392 | bytes 7340032 | tf_op jit(solution)/shard_map/dot_general | solution.py:169
  101.2 7.6 %pad_maximum_fusion = bf16[128,8,4096]{2,1,0:T(8,128)(2,1)} fusion(bf16[128,8,1024]{2,1,0:T(8,128)(2,1)} %convert_bitcast_fusion.1, bf16[128,8,3072]{2,1,0:T(8,128)(2,1)} %convert_bitcast_fusion), kind=kLoop, calls=%fused_computation.1 | loop fusion | flops 16777216 | bytes 16777216 | tf_op jit(solution)/shard_map/concatenate | solution.py:171
  108.8 5.2 %all-to-all-start.2 = ((bf16[128,8,4096]{2,1,0:T(8,128)(2,1)}), bf16[128,8,4096]{2,1,0:T(8,128)(2,1)}, u32[]{:S(2)}, u32[]{:S(2)}) async-start(bf16[128,8,4096]{2,1,0:T(8,128)(2,1)} %pad_maximum_fusion), calls=%async_computation.2 | async-start | bytes 16777216 | tf_op jit(solution)/shard_map/all_to_all | solution.py:141
  115.7 5.7 %convolution_convert_fusion.1 = bf16[128,1024]{1,0:T(8,128)(2,1)} fusion(bf16[1024,3072]{1,0:T(8,128)(2,1)} %param.15, bf16[128,1024]{1,0:T(8,128)(2,1)S(1)} %copy-done.4, bf16[128,1024]{1,0:T(8,128)(2,1)S(1)} %copy.38, bf16[128,1024]{1,0:T(8,128)(2,1)S(1)} %copy.37), kind=kOutput, calls=%fused_computation.6 | convolution fusion | flops 807796736 | bytes 7340032 | tf_op jit(solution)/shard_map/dot_general | solution.py:166
  121.3 96.6 %all-to-all-done.2 = bf16[128,8,4096]{2,1,0:T(8,128)(2,1)} async-done(((bf16[128,8,4096]{2,1,0:T(8,128)(2,1)}), bf16[128,8,4096]{2,1,0:T(8,128)(2,1)}, u32[]{:S(2)}, u32[]{:S(2)}) %all-to-all-start.2) | async-done | bytes 8388640 | tf_op jit(solution)/shard_map/all_to_all | solution.py:141
  218.0 4.6 %convert_reduce_fusion = f32[8,4096]{1,0:T(8,128)S(1)} fusion(bf16[128,8,4096]{2,1,0:T(8,128)(2,1)} %all-to-all-done.2), kind=kLoop, calls=%fused_computation | loop fusion | flops 8355840 | bytes 8519680 | tf_op jit(solution)/shard_map/reduce_sum | solution.py:173
  (29 shorter events, 4.4 us)
Async XLA Ops:
  0.6 9.6 %copy-start = (bf16[1024,1024]{1,0:T(8,128)(2,1)S(1)}, bf16[1024,1024]{1,0:T(8,128)(2,1)}, u32[]{:S(2)}) copy-start(bf16[1024,1024]{1,0:T(8,128)(2,1)} %param.16) | copy-start | bytes 6291460
  0.6 4.9 %copy-start.1 = (bf16[128,1024]{1,0:T(8,128)(2,1)S(1)}, bf16[128,1024]{1,0:T(8,128)(2,1)}, u32[]{:S(2)}) copy-start(bf16[128,1024]{1,0:T(8,128)(2,1)} %param.13) | copy-start | bytes 786436
  5.5 4.7 %copy-start.6 = (bf16[128,1024]{1,0:T(8,128)(2,1)S(1)}, bf16[128,1024]{1,0:T(8,128)(2,1)}, u32[]{:S(2)}) copy-start(bf16[128,1024]{1,0:T(8,128)(2,1)} %param.18) | copy-start | bytes 786436
  5.5 4.7 %copy-start.8 = (bf16[128,1024]{1,0:T(8,128)(2,1)S(1)}, bf16[128,1024]{1,0:T(8,128)(2,1)}, u32[]{:S(2)}) copy-start(bf16[128,1024]{1,0:T(8,128)(2,1)} %param.14) | copy-start | bytes 786436
  17.3 3.0 %copy-start.2 = (bf16[128,1024]{0,1:T(8,128)(2,1)S(1)}, bf16[128,1024]{0,1:T(8,128)(2,1)}, u32[]{:S(2)}) copy-start(bf16[128,1024]{0,1:T(8,128)(2,1)} %copy.33) | copy-start | bytes 786436
  17.3 3.1 %copy-start.3 = (bf16[128,1024]{0,1:T(8,128)(2,1)S(1)}, bf16[128,1024]{0,1:T(8,128)(2,1)}, u32[]{:S(2)}) copy-start(bf16[128,1024]{0,1:T(8,128)(2,1)} %copy.35) | copy-start | bytes 786436
  69.4 5.0 %copy-start.7 = (bf16[128,1024]{1,0:T(8,128)(2,1)S(1)}, bf16[128,1024]{1,0:T(8,128)(2,1)}, u32[]{:S(2)}) copy-start(bf16[128,1024]{1,0:T(8,128)(2,1)} %param.18) | copy-start | bytes 786436
  69.4 23.9 %all-to-all-start.1 = ((bf16[128,32,128]{2,1,0:T(8,128)(2,1)}), bf16[128,32,128]{2,1,0:T(8,128)(2,1)}, u32[]{:S(2)}, u32[]{:S(2)}) async-start(bf16[128,32,128]{2,1,0:T(8,128)(2,1)} %bitcast.44), calls=%async_computation.1 | async-start | bytes 2097152 | tf_op jit(solution)/shard_map/all_to_all | solution.py:141
  93.3 3.4 %copy-start.4 = (bf16[128,1024]{1,0:T(8,128)(2,1)S(1)}, bf16[128,1024]{1,0:T(8,128)(2,1)}, u32[]{:S(2)}) copy-start(bf16[128,1024]{1,0:T(8,128)(2,1)} %get-tuple-element.22) | copy-start | bytes 786436
  108.8 5.2 %copy-start.5 = (bf16[128,1024]{0,1:T(8,128)(2,1)S(1)}, bf16[128,1024]{0,1:T(8,128)(2,1)}, u32[]{:S(2)}) copy-start(bf16[128,1024]{0,1:T(8,128)(2,1)} %get-tuple-element.15) | copy-start | bytes 786436
  108.8 109.2 %all-to-all-start.2 = ((bf16[128,8,4096]{2,1,0:T(8,128)(2,1)}), bf16[128,8,4096]{2,1,0:T(8,128)(2,1)}, u32[]{:S(2)}, u32[]{:S(2)}) async-start(bf16[128,8,4096]{2,1,0:T(8,128)(2,1)} %pad_maximum_fusion), calls=%async_computation.2 | async-start | bytes 16777216 | tf_op jit(solution)/shard_map/all_to_all | solution.py:141

commit v2 on v1

--- a/solution.py
+++ b/solution.py
@@ -14,9 +14,12 @@
 LANES = 128
 BF = jnp.bfloat16
 F32 = jnp.float32
-VALUE, GATE_ONE, CONV_ONE, FILTER_ONE, FILTER_TWO, GRAD_CONV_TWO = range(6)
+CONV_ONE, FILTER_TWO, GATE_ONE, GRAD_CONV_TWO, FILTER_ONE, VALUE = range(6)
+GRAD_GATE_ONE, FILTER_TWO_GRAD, GRAD_VALUE, FILTER_ONE_GRAD = range(4)
 FIELDS_IN = 6
 FIELDS_OUT = 4
+WAVE = 2 * CH
+MESH = pl.DeviceIdType.MESH
 
 
 def dft_tables():
@@ -73,22 +76,86 @@
     return out[:128].astype(BF).astype(F32), out[128:].astype(BF).astype(F32)
 
 
-def local_kernel(factor, x_ref, fwd, inv, line, line_back, turn, o_ref, wide, narrow):
-    wide[...] = x_ref[...].astype(F32)
+def peer_of(step):
+    major, minor = lax.axis_index("major"), lax.axis_index("minor")
+    x = (minor // 2) % 2 * 2 + major // 4
+    x = (x + (step // 2) % 4) % 4
+    y = (major % 4 + (step // 8) % 4) % 4
+    z = (minor // 4 + step // 32) % 4
+    core = (minor + step) % 2
+    return (x % 2 * 4 + y, z * 4 + x // 2 * 2 + core)
+
+
+def my_index():
+    return lax.axis_index("major") * 16 + lax.axis_index("minor")
+
+
+def greet_all():
+    barrier = pltpu.get_barrier_semaphore()
+
+    def signal(step, carry):
+        pl.semaphore_signal(barrier, inc=1, device_id=peer_of(step), device_id_type=MESH)
+        return carry
+
+    lax.fori_loop(1, DEV, signal, 0)
+    pl.semaphore_wait(barrier, DEV - 1)
+
+
+def send_wave(src, dst, send_sem, recv_sem, own_sem):
+    me = my_index()
+    pltpu.make_async_copy(src.at[me], dst.at[me], own_sem).start()
+
+    def send(step, carry):
+        major, minor = peer_of(step)
+        pltpu.make_async_remote_copy(
+            src_ref=src.at[major * 16 + minor],
+            dst_ref=dst.at[me],
+            send_sem=send_sem,
+            recv_sem=recv_sem,
+            device_id=(major, minor),
+            device_id_type=MESH,
+        ).start()
+        return carry
+
+    lax.fori_loop(1, DEV, send, 0)
+
+
+def wait_wave(src, dst, sem, own_sem=None):
+    if own_sem is not None:
+        me = my_index()
+        pltpu.make_async_copy(src.at[me], dst.at[me], own_sem).wait()
+    most = pl.ds(0, DEV - 1)
+    pltpu.make_async_copy(src.at[most], dst.at[most], sem).wait()
+
+
+def local_kernel(
+    factor, x0, x1, x2, fwd, inv, line, line_back, turn, o0, o1,
+    r0, r1, r2, b0, b1, wide, narrow, send_sems, recv_sems, own_sems,
+):
     refs = (fwd, inv, line, line_back, turn)
+    greet_all()
+    waves = ((x0, r0), (x1, r1), (x2, r2))
+    for k, (src, dst) in enumerate(waves):
+        send_wave(src, dst, send_sems.at[k], recv_sems.at[k], own_sems.at[k])
+
+    def receive(k):
+        src, dst = waves[k]
+        wait_wave(src, dst, recv_sems.at[k], own_sems.at[k])
+        wide[k] = dst[...].astype(F32).reshape(DEV * WAVE, LANES)
 
     def pull(field, c):
+        start = field % 2 * CH + c
         return jnp.concatenate(
-            [wide[pl.ds(field * CH + c + h, DEV, FIELDS_IN * CH), :] for h in range(2)], axis=1
+            [wide[field // 2, pl.ds(start + h, DEV, WAVE), :] for h in range(2)], axis=1
         )
 
     def push(field, c, data):
         for h in range(2):
-            narrow[pl.ds(field * CH + c + h, DEV, FIELDS_OUT * CH), :] = data[
+            narrow[field // 2, pl.ds(field % 2 * CH + c + h, DEV, WAVE), :] = data[
                 :, h * 128 : h * 128 + 128
             ]
 
-    def step(i, carry):
+    def first(i, carry):
         c = 2 * i
         gate, conv = pull(GATE_ONE, c), pull(CONV_ONE, c)
         first_out = round_mul(gate, conv)
@@ -98,39 +165,64 @@
             refs,
             factor,
         )
-        push(1, c, round_mul(grad_first, conv))
-        push(3, c, filter_two_grad)
+        push(GRAD_GATE_ONE, c, round_mul(grad_first, conv))
+        push(FILTER_TWO_GRAD, c, filter_two_grad)
+        for h in range(2):
+            wide[1, pl.ds(GATE_ONE % 2 * CH + c + h, DEV, WAVE), :] = round_mul(grad_first, gate)[
+                :, h * 128 : h * 128 + 128
+            ]
+        return carry
+
+    def second(i, carry):
+        c = 2 * i
         grad_value, filter_one_grad = correlations(
-            round_mul(grad_first, gate),
+            pull(GATE_ONE, c),
             jnp.concatenate([pull(FILTER_ONE, c), pull(VALUE, c)], axis=0),
             refs,
             factor,
         )
-        push(0, c, grad_value)
-        push(2, c, filter_one_grad)
-        return carry
-
-    lax.fori_loop(0, CH // 2, step, 0)
-    o_ref[...] = narrow[...].astype(BF)
-
-
-def local_part(arrived, factor):
+        push(GRAD_VALUE, c, grad_value)
+        push(FILTER_ONE_GRAD, c, filter_one_grad)
+        return carry
+
+    receive(0)
+    receive(1)
+    lax.fori_loop(0, CH // 2, first, 0)
+    b0[...] = narrow[0].astype(BF).reshape(DEV, WAVE, LANES)
+    send_wave(b0, o0, send_sems.at[3], recv_sems.at[3], own_sems.at[3])
+    receive(2)
+    lax.fori_loop(0, CH // 2, second, 0)
+    b1[...] = narrow[1].astype(BF).reshape(DEV, WAVE, LANES)
+    send_wave(b1, o1, send_sems.at[4], recv_sems.at[4], own_sems.at[4])
+    for k, (src, dst) in enumerate(waves):
+        wait_wave(src, dst, send_sems.at[k])
+    for k, (src, dst) in enumerate(((b0, o0), (b1, o1)), 3):
+        wait_wave(src, dst, recv_sems.at[k], own_sems.at[k])
+        wait_wave(src, dst, send_sems.at[k])
+
+
+def local_part(fields, factor):
     tables = [jnp.asarray(t) for t in dft_tables()]
-    flat = arrived.reshape(DEV * FIELDS_IN * CH, LANES)
     vmem = pl.BlockSpec(memory_space=pltpu.VMEM)
-    out = pl.pallas_call(
+    piece = (DEV, WAVE, LANES)
+    return pl.pallas_call(
         functools.partial(local_kernel, factor),
-        out_shape=jax.ShapeDtypeStruct((DEV * FIELDS_OUT * CH, LANES), BF),
-        in_specs=[vmem] * 6,
-        out_specs=vmem,
-        scratch_shapes=[
-            pltpu.VMEM((DEV * FIELDS_IN * CH, LANES), F32),
-            pltpu.VMEM((DEV * FIELDS_OUT * CH, LANES), F32),
+        out_shape=(jax.ShapeDtypeStruct(piece, BF),) * 2,
+        in_specs=[vmem] * 8,
+        out_specs=(vmem,) * 2,
+        scratch_shapes=[pltpu.VMEM(piece, BF)] * 5
+        + [
+            pltpu.VMEM((3, DEV * WAVE, LANES), F32),
+            pltpu.VMEM((2, DEV * WAVE, LANES), F32),
+            pltpu.SemaphoreType.DMA((5,)),
+            pltpu.SemaphoreType.DMA((5,)),
+            pltpu.SemaphoreType.DMA((5,)),
         ],
-        compiler_params=pltpu.CompilerParams(vmem_limit_bytes=56 << 20),
+        compiler_params=pltpu.CompilerParams(
+            vmem_limit_bytes=56 << 20, collective_id=0, has_side_effects=True
+        ),
         name="local_part",
-    )(flat, *tables)
-    return out.reshape(DEV, FIELDS_OUT * CH, LANES)
+    )(*fields, *tables)
 
 
 def product(left, right):
@@ -156,12 +248,20 @@
     ).astype(BF)
     grad_conv_two = product(grad_second, gate_two)
     grad_gate_two = product(grad_second, conv_two)
-    fields = jnp.stack([value, gate_one, conv_one, filter_one, filter_two, grad_conv_two])
-    fields = fields.reshape(FIELDS_IN, rows, DEV, CH).transpose(2, 0, 3, 1)
-    arrived = exchange(fields.reshape(DEV, FIELDS_IN * CH, rows))
-    back = exchange(local_part(arrived, factor)).reshape(DEV, FIELDS_OUT, CH, rows)
-    back = back.transpose(1, 3, 0, 2).reshape(FIELDS_OUT, rows, width)
-    grad_value, grad_gate_one, filter_one_grad, filter_two_grad = back
+    def pieces(one, two):
+        pair = jnp.stack([one, two]).reshape(2, rows, DEV, CH).transpose(2, 0, 3, 1)
+        return pair.reshape(DEV, WAVE, rows)
+
+    def steps(pair):
+        pair = pair.reshape(DEV, 2, CH, rows).transpose(1, 3, 0, 2)
+        return pair.reshape(2, rows, width)
+
+    back = local_part(
+        (pieces(conv_one, filter_two), pieces(gate_one, grad_conv_two), pieces(filter_one, value)),
+        factor,
+    )
+    grad_gate_one, filter_two_grad = steps(back[0])
+    grad_value, filter_one_grad = steps(back[1])
     grad_proj = jnp.concatenate([grad_value, grad_gate_one, grad_gate_two], axis=1)
     in_grad = lax.dot_general(
         grad_proj, w_in, contract_last, preferred_element_type=F32

time: 226 us -> 222 us (0.982)
  Pallas kernels: 12.6 us -> 62.9 us
  blocking collectives: 36.1 us -> 0 us
  waiting for transfers between devices: 113 us -> 96.8 us
  local copies, waits for them, and re-layouts: 20.8 us -> 17 us
  starting transfers between devices: 10.2 us -> 6.49 us
  other arithmetic: 12.1 us -> 15.3 us
    pallas_call x1, Pallas kernels: 12.6 us -> 62.9 us  [local_part(): pl.pallas_call(functools.partial(local_kernel, factor), out_shape=(jax.Sh...]
    all_to_all x1 -> x0, blocking collectives: 36.1 us -> none  [exchange(): return lax.all_to_all(pieces, AXES, split_axis=0, concat_axis=0, tiled=True)]
    all_to_all x2 -> x1, waiting for transfers between devices: 113 us -> 96.8 us  [exchange(): return lax.all_to_all(pieces, AXES, split_axis=0, concat_axis=0, tiled=True)]
    unnamed x28 -> x11, local copies, waits for them, and re-layouts: 9.66 us -> 5.89 us
    all_to_all x2 -> x1, starting transfers between devices: 10.2 us -> 6.49 us  [exchange(): return lax.all_to_all(pieces, AXES, split_axis=0, concat_axis=0, tiled=True)]
    reshape x0 -> x2, other arithmetic: none -> 3.16 us  [pieces(): return pair.reshape(DEV, WAVE, rows)]
    transpose x0 -> x2, local copies, waits for them, and re-layouts: none -> 2.27 us  [steps(): pair = pair.reshape(DEV, 2, CH, rows).transpose(1, 3, 0, 2)]
  transfers between devices with their start and end apart: 2 -> 1, of which waited for: 2 -> 1; matrix products, arithmetic and copies ran while one was open for 5% -> 3% of each run, Pallas kernels for 0% -> 0%
where the time goes in v2:
time: 222 us; the launch traced here: 220 us
  waiting for transfers between devices  96.8 us (44%)
  Pallas kernels  62.9 us (28%)
  matrix products  20.8 us (9%)
  local copies, waits for them, and re-layouts  17 us (8%)
  other arithmetic  15.3 us (7%)
  starting transfers between devices  6.49 us (3%)
    all_to_all x1, waiting for transfers between devices, exchange(): return lax.all_to_all(pieces, AXES, split_axis=0, concat_axis=0, tiled=True)  96.8 us
    pallas_call x1, Pallas kernels, local_part(): pl.pallas_call(functools.partial(local_kernel, factor), out_shape=(jax.Sh...  62.9 us
    concatenate x1, other arithmetic, shards(): parts = jnp.concatenate([in_part, out_part], axis=1).astype(BF)  7.57 us
    all_to_all x1, starting transfers between devices, exchange(): return lax.all_to_all(pieces, AXES, split_axis=0, concat_axis=0, tiled=True)  6.49 us
    unnamed x11, local copies, waits for them, and re-layouts  5.89 us
    dot_general x1, matrix products, shards(): lax.dot_general(grad_proj, w_in, contract_last, preferred_element_type=F32)  5.68 us
    dot_general x1, matrix products, shards(): lax.dot_general(block_in, grad_proj, contract_first, preferred_element_ty...  5.47 us
    reduce_sum x1, other arithmetic, shards(): summed = jnp.sum(parts.astype(F32), axis=0) * scale  4.56 us
  transfers between devices with their start and end apart: 1, of which 1 were waited for; matrix products, arithmetic and copies ran while one was open for 3% of the time, Pallas kernels for 0%

profile of v2, /device:TPU:1, one launch (start us, length us, event | category | flops | bytes accessed | tf_op | source)
XLA Modules:
  0.0 220.0 jit_solution(784725350614665039)
XLA Ops:
  0.6 1.3 copy.28
  1.9 1.8 copy.34
  3.7 1.1 copy.29
  4.8 3.9 %convolution_convert_fusion = bf16[128,3072]{1,0:T(8,128)(2,1)S(1)} fusion(bf16[128,1024]{1,0:T(8,128)(2,1)} %param.13, bf16[1024,3072]{1,0:T(8,128)(2,1)} %param.15), kind=kOutput, calls=%fused_computation.3 | convolution fusion | flops 805699584 | bytes 7340032 | tf_op jit(solution)/shard_map/dot_general | solution.py:243
  8.7 0.8 fusion.8
  9.5 1.8 copy.35
  11.3 1.8 copy.31
  13.1 3.1 %convert_bitcast_fusion.1 = bf16[128,8,1024]{2,1,0:T(8,128)(2,1)} fusion(bf16[128,1024]{1,0:T(8,128)(2,1)} %param.14, bf16[128,1024]{1,0:T(8,128)(2,1)} %param.18, bf16[128,3072]{1,0:T(8,128)(2,1)S(1)} %convolution_convert_fusion), kind=kOutput, calls=%fused_computation.4 | convolution fusion | flops 270008320 | bytes 2883584 | tf_op jit(solution)/shard_map/dot_general | solution.py:270
  16.2 2.7 %fusion.1 = (bf16[128,1024]{1,0:T(8,128)(2,1)}, bf16[128,1024]{1,0:T(8,128)(2,1)}) fusion(bf16[128,3072]{1,0:T(8,128)(2,1)S(1)} %convolution_convert_fusion, bf16[128,1024]{1,0:T(8,128)(2,1)} %param.18, bf16[128,1024]{1,0:T(8,128)(2,1)} %param.14, bf16[1024,1024]{1,0:T(8,128)(2,1)S(1)} %copy-done), kind=kOutput, calls=%fused_computation.12 | convolution fusion | flops 269484032 | bytes 3407872 | tf_op jit(solution)/shard_map/dot_general | solution.py:246
  18.9 1.2 copy.32
  20.0 0.9 copy_bitcast_fusion.4.x0
  20.9 2.3 %copy_bitcast_fusion.2 = (bf16[128,16,128]{2,1,0:T(8,128)(2,1)}, bf16[128,16,128]{2,1,0:T(8,128)(2,1)}) fusion(bf16[1,128,128,8]{1,3,2,0:T(8,128)(2,1)S(1)} %bitcast.57, bf16[1,128,128,8]{1,3,2,0:T(8,128)(2,1)} %bitcast.56, bf16[1,128,128,8]{1,3,2,0:T(8,128)(2,1)} %bitcast.55, bf16[1,128,128,8]{1,3,2,0:T(8,128)(2,1)} %bitcast.54), kind=kLoop, calls=%fused_computation.20 | loop fusion | flops 524288 | bytes 2097152 | tf_op jit(solution)/shard_map/reshape | solution.py:253
  23.2 62.9 %local_part.1 = (bf16[128,16,128]{2,1,0:T(8,128)(2,1)}, bf16[128,16,128]{2,1,0:T(8,128)(2,1)}) custom-call(bf16[128,16,128]{2,1,0:T(8,128)(2,1)} %copy_bitcast_fusion.4.x0, bf16[128,16,128]{2,1,0:T(8,128)(2,1)} %get-tuple-element.23.x1, bf16[128,16,128]{2,1,0:T(8,128)(2,1)} %get-tuple-element.22.x2, bf16[512,256]{1,0:T(8,128)(2,1)} %constant.14.clone.fwd, ...), custom_call_target="tpu_custom_call" | custom-call | tf_op jit(solution)/shard_map/local_part/pallas_call | solution.py:208
  86.1 1.1 copy_bitcast_fusion.1
  87.5 1.1 copy_bitcast_fusion
  89.4 1.1 copy.40
  90.5 5.5 %convert_bitcast_fusion = bf16[128,8,3072]{2,1,0:T(8,128)(2,1)} fusion(bf16[128,1024]{1,0:T(8,128)(2,1)S(1)} %copy-done.1, bf16[128,1024]{1,0:T(8,128)(2,1)} %get-tuple-element.21, bf16[128,1024]{1,0:T(8,128)(2,1)S(1)} %copy.40, bf16[128,1024]{1,0:T(8,128)(2,1)S(1)} %copy.39), kind=kOutput, calls=%fused_computation.2 | convolution fusion | flops 810811392 | bytes 7340032 | tf_op jit(solution)/shard_map/dot_general | solution.py:269
  95.9 7.6 %pad_maximum_fusion = bf16[128,8,4096]{2,1,0:T(8,128)(2,1)} fusion(bf16[128,8,1024]{2,1,0:T(8,128)(2,1)} %convert_bitcast_fusion.1, bf16[128,8,3072]{2,1,0:T(8,128)(2,1)} %convert_bitcast_fusion), kind=kLoop, calls=%fused_computation.1 | loop fusion | flops 16777216 | bytes 16777216 | tf_op jit(solution)/shard_map/concatenate | solution.py:271
  103.5 6.5 %all-to-all-start = ((bf16[128,8,4096]{2,1,0:T(8,128)(2,1)}), bf16[128,8,4096]{2,1,0:T(8,128)(2,1)}, u32[]{:S(2)}, u32[]{:S(2)}) async-start(bf16[128,8,4096]{2,1,0:T(8,128)(2,1)} %pad_maximum_fusion), calls=%async_computation | async-start | bytes 16777216 | tf_op jit(solution)/shard_map/all_to_all | solution.py:233
  110.0 0.9 copy.41
  110.8 0.8 copy.42
  111.7 5.7 %convolution_convert_fusion.1 = bf16[128,1024]{1,0:T(8,128)(2,1)} fusion(bf16[1024,3072]{1,0:T(8,128)(2,1)} %param.15, bf16[128,1024]{1,0:T(8,128)(2,1)S(1)} %copy-done.2, bf16[128,1024]{1,0:T(8,128)(2,1)S(1)} %copy.40, bf16[128,1024]{1,0:T(8,128)(2,1)S(1)} %copy.39), kind=kOutput, calls=%fused_computation.5 | convolution fusion | flops 807796736 | bytes 7340032 | tf_op jit(solution)/shard_map/dot_general | solution.py:266
  117.4 96.8 %all-to-all-done = bf16[128,8,4096]{2,1,0:T(8,128)(2,1)} async-done(((bf16[128,8,4096]{2,1,0:T(8,128)(2,1)}), bf16[128,8,4096]{2,1,0:T(8,128)(2,1)}, u32[]{:S(2)}, u32[]{:S(2)}) %all-to-all-start) | async-done | bytes 8388640 | tf_op jit(solution)/shard_map/all_to_all | solution.py:233
  214.1 4.6 %convert_reduce_fusion = f32[8,4096]{1,0:T(8,128)S(1)} fusion(bf16[128,8,4096]{2,1,0:T(8,128)(2,1)} %all-to-all-done), kind=kLoop, calls=%fused_computation | loop fusion | flops 8355840 | bytes 8519680 | tf_op jit(solution)/shard_map/reduce_sum | solution.py:273
  (12 shorter events, 2.2 us)
Async XLA Ops:
  0.6 15.6 %copy-start = (bf16[1024,1024]{1,0:T(8,128)(2,1)S(1)}, bf16[1024,1024]{1,0:T(8,128)(2,1)}, u32[]{:S(2)}) copy-start(bf16[1024,1024]{1,0:T(8,128)(2,1)} %param.16) | copy-start | bytes 6291460
  18.9 71.6 %copy-start.1 = (bf16[128,1024]{1,0:T(8,128)(2,1)S(1)}, bf16[128,1024]{1,0:T(8,128)(2,1)}, u32[]{:S(2)}) copy-start(bf16[128,1024]{1,0:T(8,128)(2,1)} %param.13) | copy-start | bytes 786436
  103.5 8.2 %copy-start.2 = (bf16[128,1024]{1,0:T(8,128)(2,1)S(1)}, bf16[128,1024]{1,0:T(8,128)(2,1)}, u32[]{:S(2)}) copy-start(bf16[128,1024]{1,0:T(8,128)(2,1)} %get-tuple-element.21) | copy-start | bytes 786436
  103.5 110.6 %all-to-all-start = ((bf16[128,8,4096]{2,1,0:T(8,128)(2,1)}), bf16[128,8,4096]{2,1,0:T(8,128)(2,1)}, u32[]{:S(2)}, u32[]{:S(2)}) async-start(bf16[128,8,4096]{2,1,0:T(8,128)(2,1)} %pad_maximum_fusion), calls=%async_computation | async-start | bytes 16777216 | tf_op jit(solution)/shard_map/all_to_all | solution.py:233

commit v3 on v2

--- a/solution.py
+++ b/solution.py
@@ -225,12 +225,202 @@
     )(*fields, *tables)
 
 
+HALF = 512
+SHARES = {
+    (0, 0): [(0, 2, 0, 256), (1, 3, 0, 128)],
+    (0, 1): [(0, 2, 256, 128), (1, 3, 128, 256)],
+    (0, 2): [(0, 2, 384, 128), (1, 3, 384, 128)],
+    (1, 0): [(0, 0, 0, 128), (0, 1, 0, 128)],
+    (1, 1): [(0, 0, 128, 128), (0, 1, 128, 256)],
+    (1, 2): [(0, 0, 256, 256), (0, 1, 384, 128)],
+}
+ORDERS = (("y", "z", "x"), ("z", "x", "y"), ("x", "y", "z"))
+UNITS = [(w, g) for w in range(2) for g in range(3)]
+
+
+def width_of(unit):
+    return sum(share[3] for share in SHARES[unit])
+
+
+def coordinates():
+    major, minor = lax.axis_index("major"), lax.axis_index("minor")
+    x = (minor // 2) % 2 * 2 + major // 4
+    return {"x": x, "y": major % 4, "z": minor // 4, "core": minor % 2}
+
+
+def device_at(at):
+    return (at["x"] % 2 * 4 + at["y"], at["z"] * 4 + at["x"] // 2 * 2 + at["core"])
+
+
+def moved(at, dim, step):
+    return dict(at, **{dim: (at[dim] + step) % (2 if dim == "core" else 4)})
+
+
+def rows_at(phase, group, value):
+    every = slice(None)
+    if group == 0:
+        return [(every, value), (every, value), (value % 2, value // 2)][phase]
+    if group == 1:
+        return [(every, every, value), (value % 2, every, value // 2), (value,)][phase]
+    return [(value % 2, every, every, value // 2), (value,), (value,)][phase]
+
+
+SUMMED = (
+    ((2, 4, 2), (2, 2), ()),
+    ((2, 4, 2), (4,), ()),
+    ((4, 4), (4,), ()),
+)
+
+
+def weight_kernel(
+    scale, a1, a2, b0, b1, b2, b3, in_ref, out_ref,
+    left, left_peer, right_peer, own, got, sums, parts, last,
+    pair_sems, send_sems, recv_sems, final_sems,
+):
+    at = coordinates()
+    core = at["core"]
+    partner = device_at(moved(at, "core", 1))
+    barrier = pltpu.get_barrier_semaphore()
+    peers = [partner] + [device_at(moved(at, d, k)) for d in "xyz" for k in (1, 2, 3)]
+    for peer in peers:
+        pl.semaphore_signal(barrier, inc=1, device_id=peer, device_id_type=MESH)
+    pl.semaphore_wait(barrier, len(peers))
+
+    theirs = pl.ds(pl.multiple_of((1 - core) * HALF, HALF), HALF)
+    mine = pl.ds(pl.multiple_of(core * HALF, HALF), HALF)
+    copies = []
+
+    def remote(src, dst, send_sem, recv_sem, device):
+        copy = pltpu.make_async_remote_copy(
+            src_ref=src, dst_ref=dst, send_sem=send_sem, recv_sem=recv_sem,
+            device_id=device, device_id_type=MESH,
+        )
+        copy.start()
+        copies.append(copy)
+        return copy
+
+    pair = [
+        remote(src, dst, pair_sems.at[0, k], pair_sems.at[1, k], partner)
+        for k, (src, dst) in enumerate(
+            [(a1, left_peer.at[0]), (b2.at[:, theirs], right_peer.at[2])]
+            + [(a2, left_peer.at[1]), (b3.at[:, theirs], right_peer.at[3])]
+            + [(b0.at[:, theirs], right_peer.at[0]), (b1.at[:, theirs], right_peer.at[1])]
+        )
+    ]
+    shape = (2, 4, 4, 2, 16, 128)
+    for k, ref in enumerate((a1, a2)):
+        left[k, :, :, :, :, :, :128] = ref[...].T.reshape(shape)
+    for k in range(2):
+        pair[2 * k].wait_recv()
+        left[k, :, :, :, :, :, 128:] = left_peer[k].T.reshape(shape)
+
+    rights = (b0, b1, b2, b3)
+    arrived = {2: 1, 3: 3, 0: 4, 1: 5}
+    waited = set()
+    for u, unit in enumerate(UNITS):
+        group = unit[1]
+        dim = ORDERS[group][0]
+        for step in (2, 1, 3, 0):
+            index = rows_at(0, group, (at[dim] + step) % 4)
+            col = 0
+            for which, block, first, width in SHARES[unit]:
+                if block not in waited:
+                    waited.add(block)
+                    pair[arrived[block]].wait_recv()
+                rows = left[(which,) + index].reshape(256, 256)
+                cols = pl.ds(pl.multiple_of(core * HALF + first, 128), width)
+                right = jnp.concatenate(
+                    [rights[block][:, cols], right_peer[block, :, first : first + width]], axis=0
+                )
+                own[u][step, ..., col : col + width] = (
+                    jnp.dot(rows, right, preferred_element_type=F32)
+                    .astype(BF)
+                    .reshape(SUMMED[group][0] + (16, width))
+                )
+                col += width
+            if step:
+                remote(
+                    own[u].at[step], got[u][0].at[step - 1], send_sems.at[u, 0, step - 1],
+                    recv_sems.at[u, 0, step - 1], device_at(moved(at, dim, step)),
+                )
+    for phase in range(3):
+        for u, unit in enumerate(UNITS):
+            group = unit[1]
+            base = own[u].at[0] if phase == 0 else sums[u][phase - 1]
+            index = () if phase == 0 else rows_at(phase, group, at[ORDERS[group][phase]])
+            total = base[index + (Ellipsis,)].astype(F32)
+            for k in range(3):
+                pltpu.make_async_copy(
+                    got[u][phase].at[k], got[u][phase].at[k], recv_sems.at[u, phase, k]
+                ).wait()
+                total = total + got[u][phase][k].astype(F32)
+            if phase == 2:
+                parts[u][...] = (total * scale).reshape(2, 8, width_of(unit))
+                remote(
+                    parts[u].at[1 - core], last[u], final_sems.at[0, u], final_sems.at[1, u], partner
+                )
+                continue
+            sums[u][phase][...] = total.astype(BF)
+            dim = ORDERS[group][phase + 1]
+            for step in (2, 1, 3):
+                index = rows_at(phase + 1, group, (at[dim] + step) % 4)
+                remote(
+                    sums[u][phase].at[index], got[u][phase + 1].at[step - 1],
+                    send_sems.at[u, phase + 1, step - 1], recv_sems.at[u, phase + 1, step - 1],
+                    device_at(moved(at, dim, step)),
+                )
+    for u, unit in enumerate(UNITS):
+        pltpu.make_async_copy(last[u], last[u], final_sems.at[1, u]).wait()
+        col = 0
+        for which, block, first, width in SHARES[unit]:
+            target, start = (out_ref, 0) if which else (in_ref, block * 2 * HALF)
+            for part, half in ((parts[u].at[core], core), (last[u], 1 - core)):
+                cols = pl.ds(pl.multiple_of(start + half * HALF + first, 128), width)
+                target[:, cols] = part[:, col : col + width]
+            col += width
+    for copy in copies:
+        copy.wait_send()
+
+
+def weight_grads(block_in, second_out, blocks, scale):
+    vmem = pl.BlockSpec(memory_space=pltpu.VMEM)
+    width = block_in.shape[1]
+    own, got, sums, parts, last = [], [], [], [], []
+    for unit in UNITS:
+        w = width_of(unit)
+        shapes = [shape + (16, w) for shape in SUMMED[unit[1]]]
+        own.append(pltpu.VMEM((4,) + shapes[0], BF))
+        got.append([pltpu.VMEM((3,) + shape, BF) for shape in shapes])
+        sums.append([pltpu.VMEM(shape, BF) for shape in shapes[:2]])
+        parts.append(pltpu.VMEM((2, 8, w), F32))
+        last.append(pltpu.VMEM((8, w), F32))
+    return pl.pallas_call(
+        functools.partial(weight_kernel, scale),
+        out_shape=(
+            jax.ShapeDtypeStruct((width // DEV, 3 * width), F32),
+            jax.ShapeDtypeStruct((width // DEV, width), F32),
+        ),
+        in_specs=[vmem] * 6,
+        out_specs=(vmem,) * 2,
+        scratch_shapes=[
+            pltpu.VMEM((2, 2, 4, 4, 2, 16, 256), BF),
+            pltpu.VMEM((2, 128, width), BF),
+            pltpu.VMEM((4, 128, HALF), BF),
+            own, got, sums, parts, last,
+            pltpu.SemaphoreType.DMA((2, 6)),
+            pltpu.SemaphoreType.DMA((6, 3, 3)),
+            pltpu.SemaphoreType.DMA((6, 3, 3)),
+            pltpu.SemaphoreType.DMA((2, 6)),
+        ],
+        compiler_params=pltpu.CompilerParams(
+            vmem_limit_bytes=56 << 20, collective_id=1, has_side_effects=True
+        ),
+        name="weight_grads",
+    )(block_in, second_out, *blocks)
+
+
 def product(left, right):
     return (left.astype(F32) * right.astype(F32)).astype(BF)
-
-
-def exchange(pieces):
-    return lax.all_to_all(pieces, AXES, split_axis=0, concat_axis=0, tiled=True)
 
 
 def shards(block_in, out_cot, w_in, w_out, conv_one, conv_two, filter_one, filter_two):
@@ -239,7 +429,6 @@
     scale = seq_len ** (-0.5)
     factor = scale / (2.0 * seq_len)
     contract_last = (((1,), (1,)), ((), ()))
-    contract_first = (((0,), (0,)), ((), ()))
     proj = jnp.dot(block_in, w_in, preferred_element_type=F32).astype(BF)
     value, gate_one, gate_two = (proj[:, i * width : (i + 1) * width] for i in range(3))
     second_out = product(gate_two, conv_two)
@@ -266,18 +455,10 @@
     in_grad = lax.dot_general(
         grad_proj, w_in, contract_last, preferred_element_type=F32
     ).astype(BF)
-    in_part = lax.dot_general(block_in, grad_proj, contract_first, preferred_element_type=F32)
-    out_part = lax.dot_general(second_out, out_cot, contract_first, preferred_element_type=F32)
-    parts = jnp.concatenate([in_part, out_part], axis=1).astype(BF)
-    parts = exchange(parts.reshape(DEV, width // DEV, 4 * width))
-    summed = jnp.sum(parts.astype(F32), axis=0) * scale
-    return (
-        in_grad,
-        summed[:, : 3 * width],
-        summed[:, 3 * width :],
-        filter_one_grad,
-        filter_two_grad,
+    in_part, out_part = weight_grads(
+        block_in, second_out, (grad_value, grad_gate_one, grad_gate_two, out_cot), scale
     )
+    return (in_grad, in_part, out_part, filter_one_grad, filter_two_grad)
 
 
 def solution(mesh):

time: 222 us -> 131 us (0.59)
  waiting for transfers between devices: 96.8 us -> 0 us
  Pallas kernels: 62.9 us -> 102 us
  other arithmetic: 15.3 us -> 3.11 us
  matrix products: 20.8 us -> 12.1 us
  starting transfers between devices: 6.49 us -> 0 us
  local copies, waits for them, and re-layouts: 17 us -> 13.1 us
    all_to_all x1 -> x0, waiting for transfers between devices: 96.8 us -> none  [exchange(): return lax.all_to_all(pieces, AXES, split_axis=0, concat_axis=0, tiled=True)]
    pallas_call x0 -> x1, Pallas kernels: none -> 39 us  [weight_grads(): pl.pallas_call(functools.partial(weight_kernel, scale), out_shape=(jax.Sh...]
    dot_general x2 -> x0, matrix products: 8.55 us -> none  [the longest x1 5.47 us: shards(): lax.dot_general(block_in, grad_proj, contract_first, preferred_element_ty...]
    concatenate x1 -> x0, other arithmetic: 7.57 us -> none  [shards(): parts = jnp.concatenate([in_part, out_part], axis=1).astype(BF)]
    all_to_all x1 -> x0, starting transfers between devices: 6.49 us -> none  [exchange(): return lax.all_to_all(pieces, AXES, split_axis=0, concat_axis=0, tiled=True)]
    reduce_sum x1 -> x0, other arithmetic: 4.56 us -> none  [shards(): summed = jnp.sum(parts.astype(F32), axis=0) * scale]
    unnamed x11 -> x23, local copies, waits for them, and re-layouts: 5.89 us -> 7.2 us
  transfers between devices with their start and end apart: 1 -> 0, of which waited for: 1 -> 0; matrix products, arithmetic and copies ran while one was open for 3% -> 0% of each run, Pallas kernels for 0% -> 0%
where the time goes in v3:
time: 131 us
  Pallas kernels  102 us (78%)
  local copies, waits for them, and re-layouts  13.1 us (10%)
  matrix products  12.1 us (9%)
  other arithmetic  3.11 us (2%)
    pallas_call x1, Pallas kernels, local_part(): pl.pallas_call(functools.partial(local_kernel, factor), out_shape=(jax.Sh...  63 us
    pallas_call x1, Pallas kernels, weight_grads(): pl.pallas_call(functools.partial(weight_kernel, scale), out_shape=(jax.Sh...  39 us
    unnamed x23, local copies, waits for them, and re-layouts  7.2 us
    dot_general x1, matrix products, shards(): lax.dot_general(grad_proj, w_in, contract_last, preferred_element_type=F32)  5.82 us
    dot_general x1, matrix products, shards(): proj = jnp.dot(block_in, w_in, preferred_element_type=F32).astype(BF)  3.82 us
    reshape x2, other arithmetic, pieces(): return pair.reshape(DEV, WAVE, rows)  3.11 us
    slice x3, local copies, waits for them, and re-layouts, shards(): proj[:, i * width:(i + 1) * width]  2.7 us

profile of v3, /device:TPU:1, one launch (start us, length us, event | category | flops | bytes accessed | tf_op | source)
XLA Modules:
  0.0 131.1 jit_solution(75177885544264608)
XLA Ops:
  0.6 0.0 copy-start
  0.6 0.0 copy-start.1
  0.7 1.3 copy.24
  1.9 1.8 %copy.30 = bf16[128,1024]{0,1:T(8,128)(2,1)} copy(bf16[128,1024]{1,0:T(8,128)(2,1)} %param.19) | data formatting | bytes 524288 | tf_op args[6]
  3.7 1.1 copy.25
  4.9 0.9 copy_bitcast_fusion.4.x0
  5.8 0.0 copy-done.1
  5.8 3.8 %convolution_convert_fusion = bf16[128,3072]{1,0:T(8,128)(2,1)S(1)} fusion(bf16[128,1024]{1,0:T(8,128)(2,1)S(1)} %copy-done.1, bf16[1024,3072]{1,0:T(8,128)(2,1)} %param.15), kind=kOutput, calls=%fused_computation | convolution fusion | flops 805699584 | bytes 7340032 | tf_op jit(solution)/shard_map/dot_general | solution.py:432
  9.6 0.7 fusion.10
  10.3 0.8 copy.31
  11.2 2.5 %fusion.8 = (bf16[128,1024]{1,0:T(8,128)(2,1)}, bf16[128,1024]{1,0:T(8,128)(2,1)S(1)}, bf16[128,1024]{1,0:T(8,128)(2,1)}) fusion(bf16[128,1024]{1,0:T(8,128)(2,1)} %param.18, bf16[128,3072]{1,0:T(8,128)(2,1)S(1)} %convolution_convert_fusion, bf16[128,1024]{1,0:T(8,128)(2,1)S(1)} %copy-done.2, bf16[1024,1024]{1,0:T(8,128)(2,1)S(1)} %copy-done), kind=kOutput, calls=%fused_computation.14 | convolution fusion | flops 269746176 | bytes 3670016 | tf_op jit(solution)/shard_map/dot_general | solution.py:435
  13.7 0.2 copy.28
  13.9 1.1 copy.27
  15.0 2.2 %copy_bitcast_fusion.2 = (bf16[128,16,128]{2,1,0:T(8,128)(2,1)}, bf16[128,16,128]{2,1,0:T(8,128)(2,1)}) fusion(bf16[1,128,128,8]{1,3,2,0:T(8,128)(2,1)S(1)} %bitcast.48, bf16[1,128,128,8]{1,3,2,0:T(8,128)(2,1)S(1)} %bitcast.49, bf16[1,128,128,8]{1,3,2,0:T(8,128)(2,1)} %bitcast.47, bf16[1,128,128,8]{1,3,2,0:T(8,128)(2,1)} %bitcast.46), kind=kLoop, calls=%fused_computation.20 | loop fusion | flops 524288 | bytes 2097152 | tf_op jit(solution)/shard_map/reshape | solution.py:442
  17.2 63.0 %local_part.1 = (bf16[128,16,128]{2,1,0:T(8,128)(2,1)}, bf16[128,16,128]{2,1,0:T(8,128)(2,1)}) custom-call(bf16[128,16,128]{2,1,0:T(8,128)(2,1)} %copy_bitcast_fusion.4.x0, bf16[128,16,128]{2,1,0:T(8,128)(2,1)} %get-tuple-element.28.x1, bf16[128,16,128]{2,1,0:T(8,128)(2,1)} %get-tuple-element.27.x2, bf16[512,256]{1,0:T(8,128)(2,1)} %constant.10.clone.fwd, ...), custom_call_target="tpu_custom_call" | custom-call | tf_op jit(solution)/shard_map/local_part/pallas_call | solution.py:208
  80.2 1.2 copy_bitcast_fusion.1
  81.5 0.9 copy.39
  82.3 0.9 copy.35.b0
  83.3 0.9 copy.40
  84.1 0.9 copy.36.b1
  85.0 39.0 %weight_grads.1 = (f32[8,3072]{1,0:T(8,128)}, f32[8,1024]{1,0:T(8,128)}) custom-call(bf16[128,1024]{1,0:T(8,128)(2,1)} %a1.1, bf16[128,1024]{1,0:T(8,128)(2,1)} %get-tuple-element.18.a2, bf16[128,1024]{1,0:T(8,128)(2,1)} %copy.35.b0, bf16[128,1024]{1,0:T(8,128)(2,1)} %copy.36.b1, bf16[128,1024]{1,0:T(8,128)(2,1)} %get-tuple-element.20.b2, bf16[128,1024]{1,0:T(8,128)(2,1)} %b3.1), custom_call_target="tpu_custom_call" | custom-call | tf_op jit(solution)/shard_map/weight_grads/pallas_call | solution.py:397
  124.0 5.8 %convolution_convert_fusion.1 = bf16[128,1024]{1,0:T(8,128)(2,1)} fusion(bf16[1024,3072]{1,0:T(8,128)(2,1)} %param.15, bf16[128,1024]{1,0:T(8,128)(2,1)S(1)} %copy-done.3, bf16[128,1024]{1,0:T(8,128)(2,1)} %copy.36.b1, bf16[128,1024]{1,0:T(8,128)(2,1)S(1)} %copy-done.4), kind=kOutput, calls=%fused_computation.1 | convolution fusion | flops 807796736 | bytes 7340032 | tf_op jit(solution)/shard_map/dot_general | solution.py:455
  129.8 0.6 copy.48
  130.5 0.6 copy.49
  (16 shorter events, 0.1 us)
Async XLA Ops:
  0.6 10.5 %copy-start = (bf16[1024,1024]{1,0:T(8,128)(2,1)S(1)}, bf16[1024,1024]{1,0:T(8,128)(2,1)}, u32[]{:S(2)}) copy-start(bf16[1024,1024]{1,0:T(8,128)(2,1)} %param.16) | copy-start | bytes 6291460
  0.6 5.1 %copy-start.1 = (bf16[128,1024]{1,0:T(8,128)(2,1)S(1)}, bf16[128,1024]{1,0:T(8,128)(2,1)}, u32[]{:S(2)}) copy-start(bf16[128,1024]{1,0:T(8,128)(2,1)} %a1.1) | copy-start | bytes 786436
  5.8 5.4 %copy-start.2 = (bf16[128,1024]{1,0:T(8,128)(2,1)S(1)}, bf16[128,1024]{1,0:T(8,128)(2,1)}, u32[]{:S(2)}) copy-start(bf16[128,1024]{1,0:T(8,128)(2,1)} %b3.1) | copy-start | bytes 786436
  80.2 3.0 %copy-start.5 = (bf16[128,16,128]{2,1,0:T(8,128)(2,1)S(1)}, bf16[128,16,128]{2,1,0:T(8,128)(2,1)}, u32[]{:S(2)}) copy-start(bf16[128,16,128]{2,1,0:T(8,128)(2,1)} %get-tuple-element.10) | copy-start | bytes 1572868
  83.2 40.8 %copy-start.3 = (bf16[128,1024]{1,0:T(8,128)(2,1)S(1)}, bf16[128,1024]{1,0:T(8,128)(2,1)}, u32[]{:S(2)}) copy-start(bf16[128,1024]{1,0:T(8,128)(2,1)} %get-tuple-element.20.b2) | copy-start | bytes 786436
  83.2 40.8 %copy-start.4 = (bf16[128,1024]{1,0:T(8,128)(2,1)S(1)}, bf16[128,1024]{1,0:T(8,128)(2,1)}, u32[]{:S(2)}) copy-start(bf16[128,1024]{1,0:T(8,128)(2,1)} %copy.35.b0) | copy-start | bytes 786436
  124.0 5.8 %copy-start.6 = (f32[8,3072]{1,0:T(8,128)S(1)}, f32[8,3072]{1,0:T(8,128)}, u32[]{:S(2)}) copy-start(f32[8,3072]{1,0:T(8,128)} %get-tuple-element.35) | copy-start | bytes 294916
  124.0 6.5 %copy-start.7 = (f32[8,1024]{1,0:T(8,128)S(1)}, f32[8,1024]{1,0:T(8,128)}, u32[]{:S(2)}) copy-start(f32[8,1024]{1,0:T(8,128)} %get-tuple-element.36) | copy-start | bytes 98308

commit v4 on v2

v4 whole, which is shorter than its diff:
```python
import functools

import jax
import jax.numpy as jnp
import numpy as np
from jax import lax
from jax.experimental import pallas as pl
from jax.experimental.pallas import tpu as pltpu
from jax.sharding import PartitionSpec as P

AXES = ("major", "minor")
DEV = 128
CH = 8
LANES = 128
BF = jnp.bfloat16
F32 = jnp.float32
CONV_ONE, FILTER_TWO, GATE_ONE, GRAD_CONV_TWO, FILTER_ONE, VALUE = range(6)
GRAD_GATE_ONE, FILTER_TWO_GRAD, GRAD_VALUE, FILTER_ONE_GRAD = range(4)
FIELDS_IN = 6
FIELDS_OUT = 4
WAVE = 2 * CH
MESH = pl.DeviceIdType.MESH


def dft_tables():
    k1 = np.arange(256)[:, None]
    n1 = np.arange(128)[None, :]
    a = 2.0 * np.pi * ((k1 * n1) % 256) / 256
    c, s = np.cos(a), np.sin(a)
    n2 = np.arange(128)
    b = 2.0 * np.pi * ((n2[:, None] * n2[None, :]) % 128) / 128
    cb, sb = np.cos(b), np.sin(b)
    t = 2.0 * np.pi * (k1 * n2[None, :]) / 32768
    return (
        np.block([[c, -s], [-s, -c]]).astype(BF),
        np.block([[c.T, -s.T], [s.T, c.T]]).astype(BF),
        np.block([[cb, -sb], [sb, cb]]).astype(BF),
        np.block([[cb, sb], [-sb, cb]]).astype(BF),
        np.stack([np.cos(t), np.sin(t)]).astype(np.float32),
    )


def round_mul(a, b):
    return (a * b).astype(BF).astype(F32)


def spectrum_of(data, table, line, tw_re, tw_im):
    grid = jnp.dot(table, data, preferred_element_type=F32)
    out = []
    for h in range(2):
        re = grid[:256, h * 128 : h * 128 + 128]
        im = grid[256:, h * 128 : h * 128 + 128]
        turned = jnp.concatenate([re * tw_re + im * tw_im, im * tw_re - re * tw_im], axis=1)
        out.append(jnp.dot(turned.astype(BF), line, preferred_element_type=F32))
    return out


def correlations(left, pair, refs, factor):
    fwd, inv, line, line_back, turn = refs
    tw_re, tw_im = turn[0], turn[1]
    specs = spectrum_of(left.astype(BF), fwd[:, :128], line[...], tw_re, tw_im)
    packs = spectrum_of(pair.astype(BF), fwd[...], line[...], tw_re, tw_im)
    backs_re, backs_im = [], []
    for spec, pack in zip(specs, packs):
        l_re, l_im = spec[:, :128], spec[:, 128:]
        p_re, p_im = pack[:, :128], pack[:, 128:]
        both = jnp.concatenate([l_re * p_re + l_im * p_im, l_im * p_re - l_re * p_im], axis=1)
        back = jnp.dot(both.astype(BF), line_back[...], preferred_element_type=F32)
        b_re, b_im = back[:, :128], back[:, 128:]
        backs_re.append(b_re * tw_re - b_im * tw_im)
        backs_im.append(b_re * tw_im + b_im * tw_re)
    stacked = jnp.concatenate(
        [jnp.concatenate(backs_re, axis=1), jnp.concatenate(backs_im, axis=1)], axis=0
    ).astype(BF)
    out = jnp.dot(inv[...], stacked, preferred_element_type=F32) * factor
    return out[:128].astype(BF).astype(F32), out[128:].astype(BF).astype(F32)


def peer_of(step):
    step = step * 37 % DEV
    major, minor = lax.axis_index("major"), lax.axis_index("minor")
    x = (minor // 2) % 2 * 2 + major // 4
    x = (x + (step // 2) % 4) % 4
    y = (major % 4 + (step // 8) % 4) % 4
    z = (minor // 4 + step // 32) % 4
    core = (minor + step) % 2
    return (x % 2 * 4 + y, z * 4 + x // 2 * 2 + core)


def my_index():
    return lax.axis_index("major") * 16 + lax.axis_index("minor")


def send_wave(src, dst, send_sem, recv_sem, own_sem):
    me = my_index()
    pltpu.make_async_copy(src.at[me], dst.at[me], own_sem).start()

    def send(step, carry):
        major, minor = peer_of(step)
        pltpu.make_async_remote_copy(
            src_ref=src.at[major * 16 + minor],
            dst_ref=dst.at[me],
            send_sem=send_sem,
            recv_sem=recv_sem,
            device_id=(major, minor),
            device_id_type=MESH,
        ).start()
        return carry

    lax.fori_loop(1, DEV, send, 0)


def wait_wave(src, dst, sem, own_sem=None):
    if own_sem is not None:
        me = my_index()
        pltpu.make_async_copy(src.at[me], dst.at[me], own_sem).wait()
    most = pl.ds(0, DEV - 1)
    pltpu.make_async_copy(src.at[most], dst.at[most], sem).wait()


HALF = 512
SHARES = {
    (0, 0): [(0, 2, 0, 256), (1, 3, 0, 128)],
    (0, 1): [(0, 2, 256, 128), (1, 3, 128, 256)],
    (0, 2): [(0, 2, 384, 128), (1, 3, 384, 128)],
    (1, 0): [(0, 1, 0, 128)],
    (1, 1): [(0, 1, 128, 128)],
    (1, 2): [(0, 1, 256, 256)],
    (2, 0): [(0, 0, 0, 256)],
    (2, 1): [(0, 0, 256, 128)],
    (2, 2): [(0, 0, 384, 128)],
}
ORDERS = (("y", "z", "x"), ("z", "x", "y"), ("x", "y", "z"))
UNITS = [(w, g) for w in range(3) for g in range(3)]


def width_of(unit):
    return sum(share[3] for share in SHARES[unit])


def coordinates():
    major, minor = lax.axis_index("major"), lax.axis_index("minor")
    x = (minor // 2) % 2 * 2 + major // 4
    return {"x": x, "y": major % 4, "z": minor // 4, "core": minor % 2}


def device_at(at):
    return (at["x"] % 2 * 4 + at["y"], at["z"] * 4 + at["x"] // 2 * 2 + at["core"])


def moved(at, dim, step):
    return dict(at, **{dim: (at[dim] + step) % (2 if dim == "core" else 4)})


def rows_at(phase, group, value):
    every = slice(None)
    if group == 0:
        return [(every, value), (every, value), (value % 2, value // 2)][phase]
    if group == 1:
        return [(every, every, value), (value % 2, every, value // 2), (value,)][phase]
    return [(value % 2, every, every, value // 2), (value,), (value,)][phase]


SUMMED = (
    ((2, 4, 2), (2, 2), ()),
    ((2, 4, 2), (4,), ()),
    ((4, 4), (4,), ()),
)


NT = (((1,), (1,)), ((), ()))


def product(left, right):
    return (left.astype(F32) * right.astype(F32)).astype(BF)


def kernel(
    factor, scale,
    block_in, out_cot, conv_one, conv_two, filter_one, filter_two, w_in, w_out,
    fwd, inv, line, line_back, turn,
    in_grad, in_ref, out_ref, filter_one_grad, filter_two_grad,
    weights, grad_in, value_grad, gate_one_grad, gate_two_grad, second_out, gate_one_all,
    pieces_out, pieces_in, backs_out, backs_in, wide, narrow,
    left, left_peer, right_peer, own, got, sums, parts, last,
    weight_sems, wave_send, wave_recv, wave_own, pair_sems, send_sems, recv_sems, final_sems,
    greet_sems,
):
    at = coordinates()
    core = at["core"]
    partner = device_at(moved(at, "core", 1))
    around = {d: [device_at(moved(at, d, k)) for k in (1, 2, 3)] for d in "xyz"}
    refs = (fwd, inv, line, line_back, turn)
    copies = []

    def greet(sem, devices):
        for device in devices:
            pl.semaphore_signal(sem, inc=1, device_id=device, device_id_type=MESH)

    def remote(src, dst, send_sem, recv_sem, device):
        copy = pltpu.make_async_remote_copy(
            src_ref=src, dst_ref=dst, send_sem=send_sem, recv_sem=recv_sem,
            device_id=device, device_id_type=MESH,
        )
        copy.start()
        copies.append(copy)
        return copy

    barrier = pltpu.get_barrier_semaphore()
    near = [partner] + around["x"] + around["y"] + around["z"]
    greet(barrier, near)

    loads = []
    for k in (1, 2, 3, 0):
        src = w_out if k == 3 else w_in.at[:, pl.ds(k * 1024, 1024)]
        loads.append(pltpu.make_async_copy(src, weights.at[k], weight_sems.at[k]))
        loads[-1].start()

    def put_pieces(wave, j, one, two):
        both = [part.astype(F32).T.reshape(32, CH, LANES) for part in (one, two)]
        pieces_out[wave, pl.ds(32 * j, 32)] = jnp.concatenate(both, axis=1).astype(BF)

    def columns(j):
        return slice(256 * j, 256 * j + 256)

    for j in range(4):
        put_pieces(0, j, conv_one[:, columns(j)], filter_two[:, columns(j)])
    pl.semaphore_wait(barrier, len(near))
    greet(greet_sems.at[0], around["x"])
    for load in loads[:3]:
        load.wait()
    for j in range(4):
        c = columns(j)
        gate_one = jnp.dot(block_in[...], weights[1, :, c], preferred_element_type=F32).astype(BF)
        gate_two = jnp.dot(block_in[...], weights[2, :, c], preferred_element_type=F32).astype(BF)
        grad_second = lax.dot_general(
            out_cot[...], weights[3, c, :], NT, preferred_element_type=F32
        ).astype(BF)
        gate_two_grad[:, c] = product(grad_second, conv_two[:, c])
        second_out[:, c] = product(gate_two, conv_two[:, c])
        put_pieces(1, j, gate_one, product(grad_second, gate_two))
        if j == 1:
            pl.semaphore_wait(greet_sems.at[0], 3)
            greet(greet_sems.at[1], around["y"])
    pl.semaphore_wait(greet_sems.at[1], 3)
    greet(greet_sems.at[2], [partner])
    loads[3].wait()
    for j in range(2):
        value = jnp.dot(block_in[...], weights[0, :, columns(j)], preferred_element_type=F32)
        put_pieces(2, j, filter_one[:, columns(j)], value.astype(BF))
    pl.semaphore_wait(greet_sems.at[2], 1)

    def send(k, src, dst):
        send_wave(src, dst, wave_send.at[k], wave_recv.at[k], wave_own.at[k])

    send(0, pieces_out.at[0], pieces_in.at[0])
    send(1, pieces_out.at[1], pieces_in.at[1])
    for j in range(2, 4):
        value = jnp.dot(block_in[...], weights[0, :, columns(j)], preferred_element_type=F32)
        put_pieces(2, j, filter_one[:, columns(j)], value.astype(BF))
    send(2, pieces_out.at[2], pieces_in.at[2])

    theirs = pl.ds(pl.multiple_of((1 - core) * HALF, HALF), HALF)
    rights = (value_grad, gate_one_grad, gate_two_grad, out_cot)

    def pair_up(k, src, dst):
        return remote(src, dst, pair_sems.at[0, k], pair_sems.at[1, k], partner)

    def pair_right(block):
        return pair_up(block, rights[block].at[:, theirs], right_peer.at[block])

    def start_unit(u):
        group = UNITS[u][1]
        dim = ORDERS[group][0]
        for step in (2, 1, 3, 0):
            index = rows_at(0, group, (at[dim] + step) % 4)
            col = 0
            for which, block, first, width in SHARES[UNITS[u]]:
                rows = left[(which,) + index].reshape(256, 256)
                cols = pl.ds(pl.multiple_of(core * HALF + first, 128), width)
                right = jnp.concatenate(
                    [rights[block][:, cols], right_peer[block, :, first : first + width]], axis=0
                )
                own[u][step, ..., col : col + width] = (
                    jnp.dot(rows, right, preferred_element_type=F32)
                    .astype(BF)
                    .reshape(SUMMED[group][0] + (16, width))
                )
                col += width
            if step:
                remote(
                    own[u].at[step], got[u][0].at[step - 1], send_sems.at[u, 0, step - 1],
                    recv_sems.at[u, 0, step - 1], device_at(moved(at, dim, step)),
                )

    def advance(u, phase):
        group = UNITS[u][1]
        base = own[u].at[0] if phase == 0 else sums[u][phase - 1]
        index = () if phase == 0 else rows_at(phase, group, at[ORDERS[group][phase]])
        total = base[index + (Ellipsis,)].astype(F32)
        for k in range(3):
            pltpu.make_async_copy(
                got[u][phase].at[k], got[u][phase].at[k], recv_sems.at[u, phase, k]
            ).wait()
            total = total + got[u][phase][k].astype(F32)
        if phase == 2:
            parts[u][...] = (total * scale).reshape(2, 8, width_of(UNITS[u]))
            remote(parts[u].at[1 - core], last[u], final_sems.at[0, u], final_sems.at[1, u], partner)
            return
        sums[u][phase][...] = total.astype(BF)
        dim = ORDERS[group][phase + 1]
        for step in (2, 1, 3):
            index = rows_at(phase + 1, group, (at[dim] + step) % 4)
            remote(
                sums[u][phase].at[index], got[u][phase + 1].at[step - 1],
                send_sems.at[u, phase + 1, step - 1], recv_sems.at[u, phase + 1, step - 1],
                device_at(moved(at, dim, step)),
            )

    def finish(u):
        pltpu.make_async_copy(last[u], last[u], final_sems.at[1, u]).wait()
        col = 0
        for which, block, first, width in SHARES[UNITS[u]]:
            target, start = (out_ref, 0) if which else (in_ref, block * 2 * HALF)
            for part, half in ((parts[u].at[core], core), (last[u], 1 - core)):
                cols = pl.ds(pl.multiple_of(start + half * HALF + first, 128), width)
                target[:, cols] = part[:, col : col + width]
            col += width

    def add_in_grad(grad, block):
        for j in range(4):
            part = lax.dot_general(
                grad[...], weights[block, columns(j), :], NT, preferred_element_type=F32
            )
            grad_in[:, columns(j)] = part if block == 2 else grad_in[:, columns(j)] + part

    pairs = [
        pair_up(4, block_in, left_peer.at[0]),
        pair_up(5, second_out, left_peer.at[1]),
        pair_right(2),
        pair_right(3),
    ]
    shape = (2, 4, 4, 2, 16, 128)
    for k, ref in enumerate((block_in, second_out)):
        left[k, :, :, :, :, :, :128] = ref[...].T.reshape(shape)
    for copy in pairs:
        copy.wait_recv()
    for k in range(2):
        left[k, :, :, :, :, :, 128:] = left_peer[k].T.reshape(shape)
    for u in range(3):
        start_unit(u)
    add_in_grad(gate_two_grad, 2)

    def receive(k):
        wait_wave(pieces_out.at[k], pieces_in.at[k], wave_recv.at[k], wave_own.at[k])
        wide[k] = pieces_in[k].astype(F32).reshape(DEV * WAVE, LANES)

    def pull(field, c):
        start = field % 2 * CH + c
        return jnp.concatenate(
            [wide[field // 2, pl.ds(start + h, DEV, WAVE), :] for h in range(2)], axis=1
        )

    def push(field, c, data):
        for h in range(2):
            narrow[field // 2, pl.ds(field % 2 * CH + c + h, DEV, WAVE), :] = data[
                :, h * 128 : h * 128 + 128
            ]

    def first(i, carry):
        c = 2 * i
        gate, conv = pull(GATE_ONE, c), pull(CONV_ONE, c)
        first_out = round_mul(gate, conv)
        grad_first, filter_two_part = correlations(
            pull(GRAD_CONV_TWO, c),
            jnp.concatenate([pull(FILTER_TWO, c), first_out], axis=0),
            refs,
            factor,
        )
        push(GRAD_GATE_ONE, c, round_mul(grad_first, conv))
        push(FILTER_TWO_GRAD, c, filter_two_part)
        gate_one_all[i] = round_mul(grad_first, gate)
        return carry

    def second(i, carry):
        c = 2 * i
        grad_value, filter_one_part = correlations(
            gate_one_all[i],
            jnp.concatenate([pull(FILTER_ONE, c), pull(VALUE, c)], axis=0),
            refs,
            factor,
        )
        push(GRAD_VALUE, c, grad_value)
        push(FILTER_ONE_GRAD, c, filter_one_part)
        return carry

    def send_back(k):
        backs_out[k] = narrow[k].astype(BF).reshape(DEV, WAVE, LANES)
        send(3 + k, backs_out.at[k], backs_in.at[k])

    def take_back(k, one, two):
        wait_wave(backs_out.at[k], backs_in.at[k], wave_recv.at[3 + k], wave_own.at[3 + k])
        for j in range(4):
            part = backs_in[k, pl.ds(32 * j, 32)].astype(F32)
            one[:, columns(j)] = part[:, :CH].reshape(256, LANES).T.astype(BF)
            two[:, columns(j)] = part[:, CH:].reshape(256, LANES).T.astype(BF)

    receive(0)
    receive(1)
    lax.fori_loop(0, CH // 2, first, 0)
    send_back(0)
    for u in range(3):
        advance(u, 0)
    receive(2)
    lax.fori_loop(0, CH // 2, second, 0)
    send_back(1)
    for u in range(3):
        advance(u, 1)
    take_back(0, gate_one_grad, filter_two_grad)
    pair_right(1).wait_recv()
    for u in range(3, 6):
        start_unit(u)
    for u in range(3):
        advance(u, 2)
    add_in_grad(gate_one_grad, 1)
    take_back(1, value_grad, filter_one_grad)
    pair_right(0).wait_recv()
    for u in range(6, 9):
        start_unit(u)
    for u in range(3, 6):
        advance(u, 0)
    add_in_grad(value_grad, 0)
    in_grad[...] = grad_in[...].astype(BF)
    for u in range(3):
        finish(u)
    for u in range(6, 9):
        advance(u, 0)
    for phase in (1, 2):
        for u in range(3, 9):
            advance(u, phase)
    for u in range(3, 9):
        finish(u)
    for k in range(5):
        out, into = (pieces_out, pieces_in) if k < 3 else (backs_out, backs_in)
        wait_wave(out.at[k % 3], into.at[k % 3], wave_send.at[k])
    for copy in copies:
        copy.wait_send()


def shards(block_in, out_cot, w_in, w_out, conv_one, conv_two, filter_one, filter_two):
    rows, width = block_in.shape
    seq_len = rows * DEV
    scale = seq_len ** (-0.5)
    factor = scale / (2.0 * seq_len)
    tables = [jnp.asarray(t) for t in dft_tables()]
    own, got, sums, parts, last = [], [], [], [], []
    for unit in UNITS:
        w = width_of(unit)
        shapes = [shape + (16, w) for shape in SUMMED[unit[1]]]
        own.append(pltpu.VMEM((4,) + shapes[0], BF))
        got.append([pltpu.VMEM((3,) + shape, BF) for shape in shapes])
        sums.append([pltpu.VMEM(shape, BF) for shape in shapes[:2]])
        parts.append(pltpu.VMEM((2, 8, w), F32))
        last.append(pltpu.VMEM((8, w), F32))
    vmem = pl.BlockSpec(memory_space=pltpu.VMEM)
    anywhere = pl.BlockSpec(memory_space=pl.ANY)
    wave = (DEV, WAVE, LANES)
    flat = (DEV * WAVE, LANES)
    local = jax.ShapeDtypeStruct((rows, width), BF)
    dma = pltpu.SemaphoreType.DMA
    units = len(UNITS)
    return pl.pallas_call(
        functools.partial(kernel, factor, scale),
        out_shape=(
            local,
            jax.ShapeDtypeStruct((width // DEV, 3 * width), F32),
            jax.ShapeDtypeStruct((width // DEV, width), F32),
            local,
            local,
        ),
        in_specs=[vmem] * 6 + [anywhere] * 2 + [vmem] * 5,
        out_specs=(vmem,) * 5,
        scratch_shapes=[
            pltpu.VMEM((4, width, width), BF),
            pltpu.VMEM((rows, width), F32),
            pltpu.VMEM((rows, width), BF),
            pltpu.VMEM((rows, width), BF),
            pltpu.VMEM((rows, width), BF),
            pltpu.VMEM((rows, width), BF),
            pltpu.VMEM((CH // 2, DEV, 256), F32),
            pltpu.VMEM((3,) + wave, BF),
            pltpu.VMEM((3,) + wave, BF),
            pltpu.VMEM((2,) + wave, BF),
            pltpu.VMEM((2,) + wave, BF),
            pltpu.VMEM((3,) + flat, F32),
            pltpu.VMEM((2,) + flat, F32),
            pltpu.VMEM((2, 2, 4, 4, 2, 16, 256), BF),
            pltpu.VMEM((2, rows, width), BF),
            pltpu.VMEM((4, rows, HALF), BF),
            own, got, sums, parts, last,
            dma((4,)),
            dma((5,)),
            dma((5,)),
            dma((5,)),
            dma((2, 6)),
            dma((units, 3, 3)),
            dma((units, 3, 3)),
            dma((2, units)),
            pltpu.SemaphoreType.REGULAR((3,)),
        ],
        compiler_params=pltpu.CompilerParams(
            vmem_limit_bytes=60 << 20, collective_id=0, has_side_effects=True
        ),
        name="hyena_backward",
    )(block_in, out_cot, conv_one, conv_two, filter_one, filter_two, w_in, w_out, *tables)


def solution(mesh):
    rows = P(AXES, None)
    return jax.shard_map(
        shards,
        mesh=mesh,
        in_specs=(rows, rows, P(), P(), rows, rows, rows, rows),
        out_specs=(rows,) * 5,
        check_vma=False,
    )
```

time: 222 us -> 97.1 us (0.44)
  waiting for transfers between devices: 96.8 us -> 0 us
  Pallas kernels: 62.9 us -> 88.2 us
  matrix products: 20.8 us -> 0 us
  other arithmetic: 15.3 us -> 0 us
  local copies, waits for them, and re-layouts: 17 us -> 7.92 us
  starting transfers between devices: 6.49 us -> 0 us
    all_to_all x1 -> x0, waiting for transfers between devices: 96.8 us -> none  [exchange(): return lax.all_to_all(pieces, AXES, split_axis=0, concat_axis=0, tiled=True)]
    pallas_call x1, Pallas kernels: 62.9 us -> 88.2 us  [shards(): pl.pallas_call(functools.partial(kernel, factor, scale), out_shape=(local...]
    dot_general x5 -> x0, matrix products: 20.8 us -> none  [the longest x1 5.68 us: shards(): lax.dot_general(grad_proj, w_in, contract_last, preferred_element_type=F32)]
    concatenate x1 -> x0, other arithmetic: 7.57 us -> none  [shards(): parts = jnp.concatenate([in_part, out_part], axis=1).astype(BF)]
    all_to_all x1 -> x0, starting transfers between devices: 6.49 us -> none  [exchange(): return lax.all_to_all(pieces, AXES, split_axis=0, concat_axis=0, tiled=True)]
    slice x5 -> x0, local copies, waits for them, and re-layouts: 5.67 us -> none  [the longest x3 4.4 us: shards(): proj[:, i * width:(i + 1) * width]]
    reduce_sum x1 -> x0, other arithmetic: 4.56 us -> none  [shards(): summed = jnp.sum(parts.astype(F32), axis=0) * scale]
    reshape x2 -> x0, other arithmetic: 3.16 us -> none  [pieces(): return pair.reshape(DEV, WAVE, rows)]
  transfers between devices with their start and end apart: 1 -> 0, of which waited for: 1 -> 0; matrix products, arithmetic and copies ran while one was open for 3% -> 0% of each run, Pallas kernels for 0% -> 0%
where the time goes in v4:
time: 97.1 us; the launch traced here: 96.8 us
  Pallas kernels  88.2 us (91%)
  local copies, waits for them, and re-layouts  7.92 us (8%)
    pallas_call x1, Pallas kernels, shards(): pl.pallas_call(functools.partial(kernel, factor, scale), out_shape=(local...  88.2 us
    unnamed x5, local copies, waits for them, and re-layouts  7.92 us

profile of v4, /device:TPU:1, one launch (start us, length us, event | category | flops | bytes accessed | tf_op | source)
XLA Modules:
  0.0 96.8 jit_solution(17180079735038794013)
XLA Ops:
  0.6 88.2 %hyena_backward.1 = (bf16[128,1024]{1,0:T(8,128)(2,1)}, f32[8,3072]{1,0:T(8,128)}, f32[8,1024]{1,0:T(8,128)}, bf16[128,1024]{1,0:T(8,128)(2,1)}, bf16[128,1024]{1,0:T(8,128)(2,1)}) custom-call(bf16[128,1024]{1,0:T(8,128)(2,1)} %block_in.1, bf16[128,1024]{1,0:T(8,128)(2,1)} %out_cot.1, bf16[128,1024]{1,0:T(8,128)(2,1)} %conv_one.1, ...), custom_call_target="tpu_custom_call" | custom-call | tf_op jit(solution)/shard_map/hyena_backward/pallas_call | solution.py:472
  88.9 1.7 %copy.23 = bf16[128,1024]{1,0:T(8,128)(2,1)} copy(bf16[128,1024]{1,0:T(8,128)(2,1)} %get-tuple-element.10) | data formatting | bytes 524288
  90.6 1.5 %copy.24 = f32[8,3072]{1,0:T(8,128)} copy(f32[8,3072]{1,0:T(8,128)} %get-tuple-element.11) | data formatting | bytes 196608
  92.1 1.4 %copy.25 = f32[8,1024]{1,0:T(8,128)} copy(f32[8,1024]{1,0:T(8,128)} %get-tuple-element.12) | data formatting | bytes 65536
  93.5 1.7 %copy.26 = bf16[128,1024]{1,0:T(8,128)(2,1)} copy(bf16[128,1024]{1,0:T(8,128)(2,1)} %get-tuple-element.13) | data formatting | bytes 524288
  95.1 1.7 %copy.27 = bf16[128,1024]{1,0:T(8,128)(2,1)} copy(bf16[128,1024]{1,0:T(8,128)(2,1)} %get-tuple-element.14) | data formatting | bytes 524288

commit v5 on v4

--- a/solution.py
+++ b/solution.py
@@ -17,6 +17,10 @@
 CONV_ONE, FILTER_TWO, GATE_ONE, GRAD_CONV_TWO, FILTER_ONE, VALUE = range(6)
 GRAD_GATE_ONE, FILTER_TWO_GRAD, GRAD_VALUE, FILTER_ONE_GRAD = range(4)
 FIELDS_IN = 6
+EARLY = True
+UNROLL = 1
+RINGS = 6
+FIRST_AFTER = 1
 FIELDS_OUT = 4
 WAVE = 2 * CH
 MESH = pl.DeviceIdType.MESH
@@ -77,14 +81,14 @@
 
 
 def peer_of(step):
-    step = step * 37 % DEV
+    rem, div = lax.rem, lax.div
+    step = rem(step * 37, DEV)
     major, minor = lax.axis_index("major"), lax.axis_index("minor")
-    x = (minor // 2) % 2 * 2 + major // 4
-    x = (x + (step // 2) % 4) % 4
-    y = (major % 4 + (step // 8) % 4) % 4
-    z = (minor // 4 + step // 32) % 4
-    core = (minor + step) % 2
-    return (x % 2 * 4 + y, z * 4 + x // 2 * 2 + core)
+    x = rem(rem(div(minor, 2), 2) * 2 + div(major, 4) + div(step, 2), 4)
+    y = rem(rem(major, 4) + div(step, 8), 4)
+    z = rem(div(minor, 4) + div(step, 32), 4)
+    core = rem(minor + step, 2)
+    return (rem(x, 2) * 4 + y, z * 4 + div(x, 2) * 2 + core)
 
 
 def my_index():
@@ -189,7 +193,6 @@
     at = coordinates()
     core = at["core"]
     partner = device_at(moved(at, "core", 1))
-    around = {d: [device_at(moved(at, d, k)) for k in (1, 2, 3)] for d in "xyz"}
     refs = (fwd, inv, line, line_back, turn)
     copies = []
 
@@ -207,7 +210,11 @@
         return copy
 
     barrier = pltpu.get_barrier_semaphore()
-    near = [partner] + around["x"] + around["y"] + around["z"]
+    line_of = [moved(at, "x", k) for k in range(4)]
+    line_of = line_of[1:] + [moved(one, "core", 1) for one in line_of]
+    plane = [moved(moved(at, "y", j), "z", k) for j in range(4) for k in range(4) if j or k]
+    plane = [device_at(one) for one in plane]
+    near = plane + [device_at(one) for one in line_of]
     greet(barrier, near)
 
     loads = []
@@ -223,10 +230,13 @@
     def columns(j):
         return slice(256 * j, 256 * j + 256)
 
+    def send(k, src, dst):
+        send_wave(src, dst, wave_send.at[k], wave_recv.at[k], wave_own.at[k])
+
     for j in range(4):
         put_pieces(0, j, conv_one[:, columns(j)], filter_two[:, columns(j)])
     pl.semaphore_wait(barrier, len(near))
-    greet(greet_sems.at[0], around["x"])
+    greet(greet_sems.at[0], plane)
     for load in loads[:3]:
         load.wait()
     for j in range(4):
@@ -239,23 +249,12 @@
         gate_two_grad[:, c] = product(grad_second, conv_two[:, c])
         second_out[:, c] = product(gate_two, conv_two[:, c])
         put_pieces(1, j, gate_one, product(grad_second, gate_two))
-        if j == 1:
-            pl.semaphore_wait(greet_sems.at[0], 3)
-            greet(greet_sems.at[1], around["y"])
-    pl.semaphore_wait(greet_sems.at[1], 3)
-    greet(greet_sems.at[2], [partner])
+        if j == FIRST_AFTER:
+            pl.semaphore_wait(greet_sems.at[0], len(plane))
+            send(0, pieces_out.at[0], pieces_in.at[0])
+    send(1, pieces_out.at[1], pieces_in.at[1])
     loads[3].wait()
-    for j in range(2):
-        value = jnp.dot(block_in[...], weights[0, :, columns(j)], preferred_element_type=F32)
-        put_pieces(2, j, filter_one[:, columns(j)], value.astype(BF))
-    pl.semaphore_wait(greet_sems.at[2], 1)
-
-    def send(k, src, dst):
-        send_wave(src, dst, wave_send.at[k], wave_recv.at[k], wave_own.at[k])
-
-    send(0, pieces_out.at[0], pieces_in.at[0])
-    send(1, pieces_out.at[1], pieces_in.at[1])
-    for j in range(2, 4):
+    for j in range(4):
         value = jnp.dot(block_in[...], weights[0, :, columns(j)], preferred_element_type=F32)
         put_pieces(2, j, filter_one[:, columns(j)], value.astype(BF))
     send(2, pieces_out.at[2], pieces_in.at[2])
@@ -287,45 +286,96 @@
                     .reshape(SUMMED[group][0] + (16, width))
                 )
                 col += width
-            if step:
+
+    def halves(u):
+        count = SUMMED[UNITS[u][1]][0][0] // 2
+        return pl.ds(0, count), pl.ds(count, count)
+
+    def send_unit(u):
+        dim = ORDERS[UNITS[u][1]][0]
+        if u >= RINGS:
+            for step in (2, 1, 3):
                 remote(
                     own[u].at[step], got[u][0].at[step - 1], send_sems.at[u, 0, step - 1],
                     recv_sems.at[u, 0, step - 1], device_at(moved(at, dim, step)),
                 )
+            return
+        low, high = halves(u)
+        for k, (step, rows, to, slot) in enumerate(
+            ((2, low, 1, 1), (2, high, 3, 1), (1, high, 1, 0), (3, low, 3, 2))
+        ):
+            remote(
+                own[u].at[step, rows], got[u][0].at[slot, rows], send_sems.at[u, 0, k],
+                recv_sems.at[u, 0, k], device_at(moved(at, dim, to)),
+            )
+
+    def pass_on(u):
+        dim = ORDERS[UNITS[u][1]][0]
+        low, high = halves(u)
+        for k, (step, rows) in enumerate(((1, low), (3, high))):
+            came = got[u][0].at[1, rows]
+            pltpu.make_async_copy(came, came, recv_sems.at[u, 0, k]).wait()
+            mine = own[u][step, rows].astype(F32) + came[...].astype(F32)
+            own[u][step, rows] = mine.astype(BF)
+            remote(
+                own[u].at[step, rows], got[u][0].at[step - 1, rows], send_sems.at[u, 0, 4 + k],
+                recv_sems.at[u, 0, 4 + k], device_at(moved(at, dim, step)),
+            )
 
     def advance(u, phase):
         group = UNITS[u][1]
-        base = own[u].at[0] if phase == 0 else sums[u][phase - 1]
+        base = own[u].at[0] if phase == 0 else sums[u]
         index = () if phase == 0 else rows_at(phase, group, at[ORDERS[group][phase]])
         total = base[index + (Ellipsis,)].astype(F32)
-        for k in range(3):
-            pltpu.make_async_copy(
-                got[u][phase].at[k], got[u][phase].at[k], recv_sems.at[u, phase, k]
-            ).wait()
-            total = total + got[u][phase][k].astype(F32)
-        if phase == 2:
-            parts[u][...] = (total * scale).reshape(2, 8, width_of(UNITS[u]))
-            remote(parts[u].at[1 - core], last[u], final_sems.at[0, u], final_sems.at[1, u], partner)
+        if phase == 0 and u < RINGS:
+            low, high = halves(u)
+            for k, slot, rows in ((2, 0, high), (3, 2, low), (4, 0, low), (5, 2, high)):
+                came = got[u][0].at[slot, rows]
+                pltpu.make_async_copy(came, came, recv_sems.at[u, 0, k]).wait()
+            total = total + got[u][0][0].astype(F32) + got[u][0][2].astype(F32)
+        else:
+            for k in range(3):
+                came = got[u][phase].at[k]
+                pltpu.make_async_copy(came, came, recv_sems.at[u, phase, k]).wait()
+                total = total + came[...].astype(F32)
+        dim = ORDERS[group][phase + 1]
+        if phase == 0:
+            sums[u][...] = total.astype(BF)
+            for step in (2, 1, 3):
+                index = rows_at(1, group, (at[dim] + step) % 4)
+                remote(
+                    sums[u].at[index], got[u][1].at[step - 1], send_sems.at[u, 1, step - 1],
+                    recv_sems.at[u, 1, step - 1], device_at(moved(at, dim, step)),
+                )
             return
-        sums[u][phase][...] = total.astype(BF)
-        dim = ORDERS[group][phase + 1]
-        for step in (2, 1, 3):
-            index = rows_at(phase + 1, group, (at[dim] + step) % 4)
-            remote(
-                sums[u][phase].at[index], got[u][phase + 1].at[step - 1],
-                send_sems.at[u, phase + 1, step - 1], recv_sems.at[u, phase + 1, step - 1],
-                device_at(moved(at, dim, step)),
-            )
+        parts[u][...] = total.reshape(SUMMED[group][1] + (2, 8, width_of(UNITS[u])))
+        for step in (2, 1, 3, 0):
+            index = rows_at(2, group, (at[dim] + step) % 4)
+            there = moved(at, dim, step)
+            for flip in (0, 1):
+                if step or flip:
+                    to = moved(there, "core", flip)
+                    remote(
+                        parts[u].at[index + (to["core"],)], last[u].at[core * 4 + step],
+                        final_sems.at[0, u, 2 * step + flip], final_sems.at[1, u, 0], device_at(to),
+                    )
+        index = rows_at(2, group, at[dim])
+        last[u][core * 4] = parts[u][index + (core,)]
 
     def finish(u):
-        pltpu.make_async_copy(last[u], last[u], final_sems.at[1, u]).wait()
-        col = 0
-        for which, block, first, width in SHARES[UNITS[u]]:
-            target, start = (out_ref, 0) if which else (in_ref, block * 2 * HALF)
-            for part, half in ((parts[u].at[core], core), (last[u], 1 - core)):
-                cols = pl.ds(pl.multiple_of(start + half * HALF + first, 128), width)
-                target[:, cols] = part[:, col : col + width]
-            col += width
+        most = pl.ds(0, 7)
+        pltpu.make_async_copy(last[u].at[most], last[u].at[most], final_sems.at[1, u, 0]).wait()
+        for half in range(2):
+            total = last[u][4 * half]
+            for k in range(1, 4):
+                total = total + last[u][4 * half + k]
+            total = total * scale
+            col = 0
+            for which, block, first, width in SHARES[UNITS[u]]:
+                target, start = (out_ref, 0) if which else (in_ref, block * 2 * HALF)
+                cols = slice(start + half * HALF + first, start + half * HALF + first + width)
+                target[:, cols] = total[:, col : col + width]
+                col += width
 
     def add_in_grad(grad, block):
         for j in range(4):
@@ -349,6 +399,9 @@
         left[k, :, :, :, :, :, 128:] = left_peer[k].T.reshape(shape)
     for u in range(3):
         start_unit(u)
+    if EARLY:
+        for u in range(3):
+            send_unit(u)
     add_in_grad(gate_two_grad, 2)
 
     def receive(k):
@@ -398,53 +451,77 @@
         backs_out[k] = narrow[k].astype(BF).reshape(DEV, WAVE, LANES)
         send(3 + k, backs_out.at[k], backs_in.at[k])
 
-    def take_back(k, one, two):
+    def wait_back(k):
         wait_wave(backs_out.at[k], backs_in.at[k], wave_recv.at[3 + k], wave_own.at[3 + k])
+
+    def take_back(field, result):
+        start = field % 2 * CH
         for j in range(4):
-            part = backs_in[k, pl.ds(32 * j, 32)].astype(F32)
-            one[:, columns(j)] = part[:, :CH].reshape(256, LANES).T.astype(BF)
-            two[:, columns(j)] = part[:, CH:].reshape(256, LANES).T.astype(BF)
+            part = backs_in[field // 2, pl.ds(32 * j, 32)].astype(F32)[:, start : start + CH]
+            result[:, columns(j)] = part.reshape(256, LANES).T.astype(BF)
 
     receive(0)
     receive(1)
-    lax.fori_loop(0, CH // 2, first, 0)
+    if not EARLY:
+        for u in range(3):
+            send_unit(u)
+    lax.fori_loop(0, CH // 2, first, 0, unroll=UNROLL)
     send_back(0)
+    for u in range(min(3, RINGS)):
+        pass_on(u)
+    receive(2)
+    lax.fori_loop(0, CH // 2, second, 0, unroll=UNROLL)
+    send_back(1)
     for u in range(3):
         advance(u, 0)
-    receive(2)
-    lax.fori_loop(0, CH // 2, second, 0)
-    send_back(1)
-    for u in range(3):
-        advance(u, 1)
-    take_back(0, gate_one_grad, filter_two_grad)
+    wait_back(0)
+    take_back(GRAD_GATE_ONE, gate_one_grad)
     pair_right(1).wait_recv()
     for u in range(3, 6):
         start_unit(u)
+        send_unit(u)
     for u in range(3):
-        advance(u, 2)
+        advance(u, 1)
     add_in_grad(gate_one_grad, 1)
-    take_back(1, value_grad, filter_one_grad)
+    wait_back(1)
+    take_back(GRAD_VALUE, value_grad)
     pair_right(0).wait_recv()
     for u in range(6, 9):
         start_unit(u)
+        send_unit(u)
+    for u in range(3, min(6, RINGS)):
+        pass_on(u)
+    add_in_grad(value_grad, 0)
+    in_grad[...] = grad_in[...].astype(BF)
     for u in range(3, 6):
         advance(u, 0)
-    add_in_grad(value_grad, 0)
-    in_grad[...] = grad_in[...].astype(BF)
+    for u in range(6, RINGS):
+        pass_on(u)
+    for u in range(6, 9):
+        advance(u, 0)
+    for u in range(3, 6):
+        advance(u, 1)
     for u in range(3):
         finish(u)
+    take_back(FILTER_TWO_GRAD, filter_two_grad)
     for u in range(6, 9):
-        advance(u, 0)
-    for phase in (1, 2):
-        for u in range(3, 9):
-            advance(u, phase)
-    for u in range(3, 9):
+        advance(u, 1)
+    for u in range(3, 6):
         finish(u)
-    for k in range(5):
-        out, into = (pieces_out, pieces_in) if k < 3 else (backs_out, backs_in)
-        wait_wave(out.at[k % 3], into.at[k % 3], wave_send.at[k])
+    take_back(FILTER_ONE_GRAD, filter_one_grad)
+    for u in range(6, 9):
+        finish(u)
+    for k in range(3):
+        wait_wave(pieces_out.at[k], pieces_in.at[k], wave_send.at[k])
+    for k in range(2):
+        wait_wave(backs_out.at[k], backs_in.at[k], wave_send.at[3 + k])
     for copy in copies:
         copy.wait_send()
+
+
+def store_kernel(*refs):
+    for src, dst in zip(refs[:5], refs[5:]):
+        dst[...] = src[...]
 
 
 def shards(block_in, out_cot, w_in, w_out, conv_one, conv_two, filter_one, filter_two):
@@ -456,12 +533,12 @@
     own, got, sums, parts, last = [], [], [], [], []
     for unit in UNITS:
         w = width_of(unit)
-        shapes = [shape + (16, w) for shape in SUMMED[unit[1]]]
-        own.append(pltpu.VMEM((4,) + shapes[0], BF))
-        got.append([pltpu.VMEM((3,) + shape, BF) for shape in shapes])
-        sums.append([pltpu.VMEM(shape, BF) for shape in shapes[:2]])
-        parts.append(pltpu.VMEM((2, 8, w), F32))
-        last.append(pltpu.VMEM((8, w), F32))
+        first, second, _ = SUMMED[unit[1]]
+        own.append(pltpu.VMEM((4,) + first + (16, w), BF))
+        got.append([pltpu.VMEM((3,) + shape + (16, w), BF) for shape in (first, second)])
+        sums.append(pltpu.VMEM(first + (16, w), BF))
+        parts.append(pltpu.VMEM(second + (2, 8, w), F32))
+        last.append(pltpu.VMEM((8, 8, w), F32))
     vmem = pl.BlockSpec(memory_space=pltpu.VMEM)
     anywhere = pl.BlockSpec(memory_space=pl.ANY)
     wave = (DEV, WAVE, LANES)
@@ -469,15 +546,16 @@
     local = jax.ShapeDtypeStruct((rows, width), BF)
     dma = pltpu.SemaphoreType.DMA
     units = len(UNITS)
-    return pl.pallas_call(
+    outputs = (
+        local,
+        jax.ShapeDtypeStruct((width // DEV, 3 * width), F32),
+        jax.ShapeDtypeStruct((width // DEV, width), F32),
+        local,
+        local,
+    )
+    results = pl.pallas_call(
         functools.partial(kernel, factor, scale),
-        out_shape=(
-            local,
-            jax.ShapeDtypeStruct((width // DEV, 3 * width), F32),
-            jax.ShapeDtypeStruct((width // DEV, width), F32),
-            local,
-            local,
-        ),
+        out_shape=outputs,
         in_specs=[vmem] * 6 + [anywhere] * 2 + [vmem] * 5,
         out_specs=(vmem,) * 5,
         scratch_shapes=[
@@ -503,16 +581,23 @@
             dma((5,)),
             dma((5,)),
             dma((2, 6)),
-            dma((units, 3, 3)),
-            dma((units, 3, 3)),
-            dma((2, units)),
-            pltpu.SemaphoreType.REGULAR((3,)),
+            dma((units, 2, 6)),
+            dma((units, 2, 6)),
+            dma((2, units, 8)),
+            pltpu.SemaphoreType.REGULAR((1,)),
         ],
         compiler_params=pltpu.CompilerParams(
             vmem_limit_bytes=60 << 20, collective_id=0, has_side_effects=True
         ),
         name="hyena_backward",
     )(block_in, out_cot, conv_one, conv_two, filter_one, filter_two, w_in, w_out, *tables)
+    return pl.pallas_call(
+        store_kernel,
+        out_shape=outputs,
+        in_specs=[vmem] * 5,
+        out_specs=(vmem,) * 5,
+        name="store",
+    )(*results)
 
 
 def solution(mesh):

time: 97.1 us -> 80.5 us (0.83)
  Pallas kernels: 88.2 us -> 79.7 us
  local copies, waits for them, and re-layouts: 7.92 us -> 0 us
    pallas_call x1 -> x2, Pallas kernels: 88.2 us -> 79.7 us  [the longest x1 77.6 us: shards(): pl.pallas_call(functools.partial(kernel, factor, scale), out_shape=output...]
    unnamed x5 -> x0, local copies, waits for them, and re-layouts: 7.92 us -> none
where the time goes in v5:
time: 80.5 us; the launch traced here: 80.4 us
  Pallas kernels  79.7 us (99%)
    pallas_call x1, Pallas kernels, shards(): pl.pallas_call(functools.partial(kernel, factor, scale), out_shape=output...  77.6 us
    pallas_call x1, Pallas kernels, shards(): pl.pallas_call(store_kernel, out_shape=outputs, in_specs=[vmem] * 5, out_...  2.11 us

profile of v5, /device:TPU:1, one launch (start us, length us, event | category | flops | bytes accessed | tf_op | source)
XLA Modules:
  0.0 80.4 jit_solution(16093885892021225600)
XLA Ops:
  0.6 77.6 %hyena_backward.1 = (bf16[128,1024]{1,0:T(8,128)(2,1)}, f32[8,3072]{1,0:T(8,128)}, f32[8,1024]{1,0:T(8,128)}, bf16[128,1024]{1,0:T(8,128)(2,1)}, bf16[128,1024]{1,0:T(8,128)(2,1)}) custom-call(bf16[128,1024]{1,0:T(8,128)(2,1)} %block_in.1, bf16[128,1024]{1,0:T(8,128)(2,1)} %out_cot.1, bf16[128,1024]{1,0:T(8,128)(2,1)} %conv_one.1, ...), custom_call_target="tpu_custom_call" | custom-call | tf_op jit(solution)/shard_map/hyena_backward/pallas_call | solution.py:556
  78.3 2.1 %store.1 = (bf16[128,1024]{1,0:T(8,128)(2,1)}, f32[8,3072]{1,0:T(8,128)}, f32[8,1024]{1,0:T(8,128)}, bf16[128,1024]{1,0:T(8,128)(2,1)}, bf16[128,1024]{1,0:T(8,128)(2,1)}) custom-call(bf16[128,1024]{1,0:T(8,128)(2,1)} %get-tuple-element.10.refs_0_, f32[8,3072]{1,0:T(8,128)} %get-tuple-element.11.refs_1_, f32[8,1024]{1,0:T(8,128)} %get-tuple-element.12.refs_2_, ...), custom_call_target="tpu_custom_call" | custom-call | tf_op jit(solution)/shard_map/store/pallas_call | solution.py:594

commit v6 on v5

--- a/solution.py
+++ b/solution.py
@@ -18,9 +18,10 @@
 GRAD_GATE_ONE, FILTER_TWO_GRAD, GRAD_VALUE, FILTER_ONE_GRAD = range(4)
 FIELDS_IN = 6
 EARLY = True
-UNROLL = 1
+UNROLL = 2
 RINGS = 6
-FIRST_AFTER = 1
+FIRST_AFTER = 2
+NEAR_AFTER = 0
 FIELDS_OUT = 4
 WAVE = 2 * CH
 MESH = pl.DeviceIdType.MESH
@@ -235,8 +236,9 @@
 
     for j in range(4):
         put_pieces(0, j, conv_one[:, columns(j)], filter_two[:, columns(j)])
-    pl.semaphore_wait(barrier, len(near))
-    greet(greet_sems.at[0], plane)
+    if NEAR_AFTER < 0:
+        pl.semaphore_wait(barrier, len(near))
+        greet(greet_sems.at[0], plane)
     for load in loads[:3]:
         load.wait()
     for j in range(4):
@@ -249,6 +251,9 @@
         gate_two_grad[:, c] = product(grad_second, conv_two[:, c])
         second_out[:, c] = product(gate_two, conv_two[:, c])
         put_pieces(1, j, gate_one, product(grad_second, gate_two))
+        if j == NEAR_AFTER:
+            pl.semaphore_wait(barrier, len(near))
+            greet(greet_sems.at[0], plane)
         if j == FIRST_AFTER:
             pl.semaphore_wait(greet_sems.at[0], len(plane))
             send(0, pieces_out.at[0], pieces_in.at[0])
@@ -472,17 +477,15 @@
     receive(2)
     lax.fori_loop(0, CH // 2, second, 0, unroll=UNROLL)
     send_back(1)
-    for u in range(3):
-        advance(u, 0)
     wait_back(0)
     take_back(GRAD_GATE_ONE, gate_one_grad)
     pair_right(1).wait_recv()
     for u in range(3, 6):
         start_unit(u)
         send_unit(u)
+    add_in_grad(gate_one_grad, 1)
     for u in range(3):
-        advance(u, 1)
-    add_in_grad(gate_one_grad, 1)
+        advance(u, 0)
     wait_back(1)
     take_back(GRAD_VALUE, value_grad)
     pair_right(0).wait_recv()
@@ -491,6 +494,8 @@
         send_unit(u)
     for u in range(3, min(6, RINGS)):
         pass_on(u)
+    for u in range(3):
+        advance(u, 1)
     add_in_grad(value_grad, 0)
     in_grad[...] = grad_in[...].astype(BF)
     for u in range(3, 6):

time: 80.5 us -> 78.8 us (0.979)
  Pallas kernels: 79.7 us -> 78 us
    pallas_call x1, Pallas kernels: 77.6 us -> 75.9 us  [shards(): pl.pallas_call(functools.partial(kernel, factor, scale), out_shape=output...]
where the time goes in v6:
time: 78.8 us; the launch traced here: 78.6 us
  Pallas kernels  78 us (99%)
    pallas_call x1, Pallas kernels, shards(): pl.pallas_call(functools.partial(kernel, factor, scale), out_shape=output...  75.9 us
    pallas_call x1, Pallas kernels, shards(): pl.pallas_call(store_kernel, out_shape=outputs, in_specs=[vmem] * 5, out_...  2.11 us

profile of v6, /device:TPU:1, one launch (start us, length us, event | category | flops | bytes accessed | tf_op | source)
XLA Modules:
  0.0 78.6 jit_solution(17332961660609871671)
XLA Ops:
  0.6 75.9 %hyena_backward.1 = (bf16[128,1024]{1,0:T(8,128)(2,1)}, f32[8,3072]{1,0:T(8,128)}, f32[8,1024]{1,0:T(8,128)}, bf16[128,1024]{1,0:T(8,128)(2,1)}, bf16[128,1024]{1,0:T(8,128)(2,1)}) custom-call(bf16[128,1024]{1,0:T(8,128)(2,1)} %block_in.1, bf16[128,1024]{1,0:T(8,128)(2,1)} %out_cot.1, bf16[128,1024]{1,0:T(8,128)(2,1)} %conv_one.1, ...), custom_call_target="tpu_custom_call" | custom-call | tf_op jit(solution)/shard_map/hyena_backward/pallas_call | solution.py:561
  76.5 2.1 %store.1 = (bf16[128,1024]{1,0:T(8,128)(2,1)}, f32[8,3072]{1,0:T(8,128)}, f32[8,1024]{1,0:T(8,128)}, bf16[128,1024]{1,0:T(8,128)(2,1)}, bf16[128,1024]{1,0:T(8,128)(2,1)}) custom-call(bf16[128,1024]{1,0:T(8,128)(2,1)} %get-tuple-element.10.refs_0_, f32[8,3072]{1,0:T(8,128)} %get-tuple-element.11.refs_1_, f32[8,1024]{1,0:T(8,128)} %get-tuple-element.12.refs_2_, ...), custom_call_target="tpu_custom_call" | custom-call | tf_op jit(solution)/shard_map/store/pallas_call | solution.py:599

commit v7 on v6

--- a/solution.py
+++ b/solution.py
@@ -484,8 +484,6 @@
         start_unit(u)
         send_unit(u)
     add_in_grad(gate_one_grad, 1)
-    for u in range(3):
-        advance(u, 0)
     wait_back(1)
     take_back(GRAD_VALUE, value_grad)
     pair_right(0).wait_recv()
@@ -494,6 +492,8 @@
         send_unit(u)
     for u in range(3, min(6, RINGS)):
         pass_on(u)
+    for u in range(3):
+        advance(u, 0)
     for u in range(3):
         advance(u, 1)
     add_in_grad(value_grad, 0)

time: 78.8 us -> 80.9 us (1.027)
  Pallas kernels: 78 us -> 80.1 us
    pallas_call x1, Pallas kernels: 75.9 us -> 78 us  [shards(): pl.pallas_call(functools.partial(kernel, factor, scale), out_shape=output...]
where the time goes in v7:
time: 80.9 us; the launch traced here: 80.8 us
  Pallas kernels  80.1 us (99%)
    pallas_call x1, Pallas kernels, shards(): pl.pallas_call(functools.partial(kernel, factor, scale), out_shape=output...  78 us
    pallas_call x1, Pallas kernels, shards(): pl.pallas_call(store_kernel, out_shape=outputs, in_specs=[vmem] * 5, out_...  2.11 us

profile of v7, /device:TPU:1, one launch (start us, length us, event | category | flops | bytes accessed | tf_op | source)
XLA Modules:
  0.0 80.8 jit_solution(13119988989571348924)
XLA Ops:
  0.6 78.0 %hyena_backward.1 = (bf16[128,1024]{1,0:T(8,128)(2,1)}, f32[8,3072]{1,0:T(8,128)}, f32[8,1024]{1,0:T(8,128)}, bf16[128,1024]{1,0:T(8,128)(2,1)}, bf16[128,1024]{1,0:T(8,128)(2,1)}) custom-call(bf16[128,1024]{1,0:T(8,128)(2,1)} %block_in.1, bf16[128,1024]{1,0:T(8,128)(2,1)} %out_cot.1, bf16[128,1024]{1,0:T(8,128)(2,1)} %conv_one.1, ...), custom_call_target="tpu_custom_call" | custom-call | tf_op jit(solution)/shard_map/hyena_backward/pallas_call | solution.py:561
  78.7 2.1 %store.1 = (bf16[128,1024]{1,0:T(8,128)(2,1)}, f32[8,3072]{1,0:T(8,128)}, f32[8,1024]{1,0:T(8,128)}, bf16[128,1024]{1,0:T(8,128)(2,1)}, bf16[128,1024]{1,0:T(8,128)(2,1)}) custom-call(bf16[128,1024]{1,0:T(8,128)(2,1)} %get-tuple-element.10.refs_0_, f32[8,3072]{1,0:T(8,128)} %get-tuple-element.11.refs_1_, f32[8,1024]{1,0:T(8,128)} %get-tuple-element.12.refs_2_, ...), custom_call_target="tpu_custom_call" | custom-call | tf_op jit(solution)/shard_map/store/pallas_call | solution.py:599
